TPU v7x, 32 devices: a whole 2x2x4 slice. The times are simulated.
32 devices in a mesh: fsdp: 8 (over y, x, core), seq: 4 (over z).
Axes of the slice: x: 2, y: 2, z: 4, core: 2. Of those that a mesh axis runs over, the one named last changes fastest.
Arguments:
- tokens: bfloat16 [8, 2048, 768], P('fsdp', 'seq'), may hold values from -6 to 6
- cotangent: bfloat16 [8, 2048, 768], P('fsdp', 'seq'), may hold values from -6 to 6
- w_qkv: bfloat16 [768, 2304], P(('fsdp', 'seq')), may hold values from -0.3125 to 0.3125
- b_qkv: bfloat16 [2304], P(('fsdp', 'seq')), may hold values from -1.796875 to 1.796875
- w_out: bfloat16 [768, 768], P(('fsdp', 'seq')), may hold values from -0.875 to 0.875
- b_out: bfloat16 [768], P(('fsdp', 'seq')), may hold values from -1.796875 to 1.796875
- w_up: bfloat16 [768, 3072], P(('fsdp', 'seq')), may hold values from -0.21875 to 0.21875
- b_up: bfloat16 [3072], P(('fsdp', 'seq')), may hold values from -1.796875 to 1.796875
- w_down: bfloat16 [3072, 768], P(('fsdp', 'seq')), may hold values from -0.109375 to 0.109375
- b_down: bfloat16 [768], P(('fsdp', 'seq')), may hold values from -1.796875 to 1.796875
- gain_attn: bfloat16 [768], P(('fsdp', 'seq')), may hold values from 0.099609375 to 1.8984375
- shift_attn: bfloat16 [768], P(('fsdp', 'seq')), may hold values from -1.796875 to 1.796875
- gain_mlp: bfloat16 [768], P(('fsdp', 'seq')), may hold values from 0.099609375 to 1.8984375
- shift_mlp: bfloat16 [768], P(('fsdp', 'seq')), may hold values from -1.796875 to 1.796875
Outputs:
- block_out: bfloat16 [8, 2048, 768], P('fsdp', 'seq')
- grad_tokens: bfloat16 [8, 2048, 768], P('fsdp', 'seq')
- grad_w_qkv: float32 [768, 2304], P(('fsdp', 'seq'))
- grad_b_qkv: float32 [2304], P(('fsdp', 'seq'))
- grad_w_out: float32 [768, 768], P(('fsdp', 'seq'))
- grad_b_out: float32 [768], P(('fsdp', 'seq'))
- grad_w_up: float32 [768, 3072], P(('fsdp', 'seq'))
- grad_b_up: float32 [3072], P(('fsdp', 'seq'))
- grad_w_down: float32 [3072, 768], P(('fsdp', 'seq'))
- grad_b_down: float32 [768], P(('fsdp', 'seq'))
- grad_gain_attn: float32 [768], P(('fsdp', 'seq'))
- grad_shift_attn: float32 [768], P(('fsdp', 'seq'))
- grad_gain_mlp: float32 [768], P(('fsdp', 'seq'))
- grad_shift_mlp: float32 [768], P(('fsdp', 'seq'))
All inputs are finite; a program needn't handle non-finite values.
Results may differ from a plain program's by a relative error of at most 0.012.
The roundings to bfloat16 on the way count: a program that leaves them out, or rounds other values in their place, can miss the bound.
Values may be sent and summed in bfloat16 or wider, within the bound.
No kernel may reach another device: no remote copies, remote signals or barrier semaphores. Data moves between devices by JAX's collectives and lax.ppermute only.
A program may use at most 192 MiB of HBM per device.

v0:
```python
import math

import jax
import jax.numpy as jnp
from jax import lax
from jax.experimental import pallas as pl
from jax.experimental.pallas import tpu as pltpu
from jax.sharding import PartitionSpec as P

HEAD = 64
ROT = 16
mask_fill = -1e30
eps = 1e-05
BLK = 256
F32 = jnp.float32
BF = jnp.bfloat16


def rot_tables(positions):
    lane = lax.broadcasted_iota(jnp.int32, (1, 128), 1) % HEAD
    half = ROT // 2
    inv = jnp.exp((lane % half).astype(F32) * (-2.0 * math.log(10000.0) / ROT))
    ang = positions.astype(F32)[:, None] * inv
    cos, sin = jnp.cos(ang), jnp.sin(ang)
    c = jnp.where(lane < ROT, cos, 1.0)
    sa = jnp.where(lane < half, -sin, 0.0)
    sb = jnp.where((lane >= half) & (lane < ROT), sin, 0.0)
    return c, sa, sb

def nt(a, b):
    return lax.dot_general(a, b, (((1,), (1,)), ((), ())), preferred_element_type=F32)

def nn(a, b):
    return lax.dot_general(a, b, (((1,), (0,)), ((), ())), preferred_element_type=F32)

def attend(rank, proj, grad_mixed, tables):
    n, c, width = grad_mixed.shape
    heads = width // HEAD
    length = n * c
    half = ROT // 2
    nq = length // BLK
    scale = HEAD ** (-0.5)

    def kernel(rank_ref, proj_ref, gm_ref, c_ref, sa_ref, sb_ref, mixed_ref, gp_ref, sum_ref,
               q_s, k_s, v_s, d_s, dk_s, dv_s, s_s, dp_s, p_s):
        rank = rank_ref[0]

        def spin(x, at, sign):
            cc, sa, sb = c_ref[at], sa_ref[at], sb_ref[at]
            left = pltpu.roll(x, 128 - half, 1)
            right = pltpu.roll(x, half, 1)
            return x * cc + sign * (left * sa + right * sb)

        def load(chunk, carry):
            at = lax.rem(rank - chunk + n, n)
            rows = pl.ds(pl.multiple_of(chunk * c, c), c)
            for tile in range(2 * width // 128):
                x = spin(proj_ref[at, :, tile * 128:(tile + 1) * 128], at, 1.0)
                for side in range(2):
                    slot = tile * 2 + side
                    piece = x[:, side * HEAD:(side + 1) * HEAD].astype(BF)
                    if slot < heads:
                        q_s[slot, rows, :] = piece * jnp.asarray(scale, BF)
                    else:
                        k_s[slot - heads, rows, :] = piece
            for h in range(heads):
                v_s[h, rows, :] = proj_ref[at, :, 2 * width + h * HEAD:2 * width + (h + 1) * HEAD].astype(BF)
                d_s[h, rows, :] = gm_ref[at, :, h * HEAD:(h + 1) * HEAD]
            return carry
        lax.fori_loop(0, n, load, 0)

        def one_head(h, carry):
            dk_s[h] = jnp.zeros((length, HEAD), F32)
            dv_s[h] = jnp.zeros((length, HEAD), F32)
            row = lax.broadcasted_iota(jnp.int32, (BLK, BLK), 0)
            col = lax.broadcasted_iota(jnp.int32, (BLK, BLK), 1)
            tri = row <= col
            for i in range(nq):
                span = slice(i * BLK, (i + 1) * BLK)
                qi = q_s[h, span, :]
                di = d_s[h, span, :]
                top = jnp.full((8, BLK), mask_fill, F32)
                for j in range(i + 1):
                    s = nt(k_s[h, j * BLK:(j + 1) * BLK, :], qi)
                    if j == i:
                        s = jnp.where(tri, s, mask_fill)
                    s_s[j] = s
                    top = jnp.maximum(top, jnp.max(s.reshape(BLK // 8, 8, BLK), axis=0))
                top = jnp.max(top, axis=0, keepdims=True)
                tot = jnp.zeros((8, BLK), F32)
                for j in range(i + 1):
                    e = jnp.exp(s_s[j] - top)
                    s_s[j] = e
                    tot = tot + jnp.sum(e.reshape(BLK // 8, 8, BLK), axis=0)
                inv = 1.0 / jnp.sum(tot, axis=0, keepdims=True)
                out = jnp.zeros((HEAD, BLK), F32)
                delta = jnp.zeros((8, BLK), F32)
                for j in range(i + 1):
                    keys = slice(j * BLK, (j + 1) * BLK)
                    p = s_s[j] * inv
                    s_s[j] = p
                    low = p.astype(BF)
                    dp = nt(v_s[h, keys, :], di)
                    dp_s[j] = dp
                    delta = delta + jnp.sum((p * dp).reshape(BLK // 8, 8, BLK), axis=0)
                    out = out + nn(v_s[h, keys, :].T, low)
                    dv_s[h, keys, :] = dv_s[h, keys, :] + nn(low, di)
                delta = jnp.sum(delta, axis=0, keepdims=True)
                dq = jnp.zeros((HEAD, BLK), F32)
                for j in range(i + 1):
                    keys = slice(j * BLK, (j + 1) * BLK)
                    ds = (s_s[j] * (dp_s[j] - delta)).astype(BF)
                    dq = dq + nn(k_s[h, keys, :].T, ds)
                    dk_s[h, keys, :] = dk_s[h, keys, :] + nn(ds, qi)
                q_s[h, span, :] = (dq * scale).T.astype(BF)
                d_s[h, span, :] = out.T.astype(BF)
            return carry
        lax.fori_loop(0, heads, one_head, 0)

        sum_ref[...] = jnp.zeros_like(sum_ref)

        def store(chunk, carry):
            at = lax.rem(rank - chunk + n, n)
            rows = pl.ds(pl.multiple_of(chunk * c, c), c)
            for tile in range(2 * width // 128):
                pieces = []
                for side in range(2):
                    slot = tile * 2 + side
                    if slot < heads:
                        pieces.append(q_s[slot, rows, :].astype(F32))
                    else:
                        pieces.append(dk_s[slot - heads, rows, :].astype(BF).astype(F32))
                x = spin(jnp.concatenate(pieces, axis=1), at, -1.0).astype(BF)
                lanes = slice(tile * 128, (tile + 1) * 128)
                gp_ref[at, :, lanes] = x
                sum_ref[:, lanes] += jnp.sum(x.astype(F32).reshape(c // 8, 8, 128), axis=0)
            x = jnp.concatenate([dv_s[h, rows, :].astype(BF) for h in range(heads)], axis=1)
            gp_ref[at, :, 2 * width:] = x
            sum_ref[:, 2 * width:] += jnp.sum(x.astype(F32).reshape(c // 8, 8, width), axis=0)
            mixed_ref[at] = jnp.concatenate([d_s[h, rows, :] for h in range(heads)], axis=1)
            return carry
        lax.fori_loop(0, n, store, 0)

    vm = pl.BlockSpec(memory_space=pltpu.VMEM)
    flops = 6 * heads * length * length * HEAD
    return pl.pallas_call(
        kernel,
        out_shape=(
            jax.ShapeDtypeStruct((n, c, width), BF),
            jax.ShapeDtypeStruct((n, c, 3 * width), BF),
            jax.ShapeDtypeStruct((8, 3 * width), F32),
        ),
        in_specs=[pl.BlockSpec(memory_space=pltpu.SMEM)] + [vm] * 5,
        out_specs=(vm, vm, vm),
        scratch_shapes=[pltpu.VMEM((heads, length, HEAD), BF)] * 4
        + [pltpu.VMEM((heads, length, HEAD), F32)] * 2
        + [pltpu.VMEM((nq, BLK, BLK), F32)] * 2 + [pltpu.VMEM((8, 128), BF)],
        compiler_params=pltpu.CompilerParams(vmem_limit_bytes=56 << 20),
        cost_estimate=pl.CostEstimate(flops=flops, bytes_accessed=16 << 20, transcendentals=heads * length * length // 2),
        name="attend",
    )(rank, proj, grad_mixed, *tables)


def tn(a, b):
    return lax.dot_general(a, b, (((0,), (0,)), ((), ())), preferred_element_type=F32)


def normalized(x):
    centred = x - jnp.mean(x, axis=-1, keepdims=True)
    spread = lax.rsqrt(jnp.mean(centred * centred, axis=-1, keepdims=True) + eps)
    return centred * spread, spread


def half_erf(pre):
    return 0.5 * (1.0 + lax.erf(pre * math.sqrt(0.5)))


def tokens_spec(size):
    return pl.BlockSpec((None, BLK, size), lambda i, j, *_: (i, j, 0))


def whole_spec(shape):
    return pl.BlockSpec(shape, lambda i, j, *_: (0,) * len(shape))


def rows8(v):
    return jnp.sum(v.reshape(BLK // 8, 8, v.shape[1]), axis=0)


def spread_out(ref, totals, nf):
    tall, d = ref.shape[1:]
    for f in range(nf):
        at = 0
        for total in totals:
            size, wide = total.shape[0] // nf, total.shape[1]
            ref[f, at : at + size, :wide] = total[f * size : (f + 1) * size, :].astype(BF)
            if wide < d:
                ref[f, at : at + size, wide:] = jnp.zeros((size, d - wide), BF)
            at += size
        if at < tall:
            ref[f, at:, :] = jnp.zeros((tall - at, d), BF)


def feed(nf, spare, rank, toks, cots, norms, weights, b_qkv, w_out, b_up):
    n, c, d = toks.shape
    wide, width, hid = b_qkv.shape[1], w_out.shape[0], b_up.shape[1]
    last = n * (c // BLK) - 1
    tall = (d + hid) // nf + spare

    def kernel(
        rank_ref, x_ref, cot_ref, norm_ref, w_ref, bq_ref, wo_ref, bu_ref,
        proj_ref, mixed_ref, out_ref, q_ref, all_ref, sum_ref, up_ref, au, ad,
    ):
        w_up = w_ref[:, :hid]
        w_down = w_ref[:, hid : hid + d]
        w_qkv = w_ref[:, hid + d :]
        step = pl.program_id(0) * (c // BLK) + pl.program_id(1)

        @pl.when(step == 0)
        def _():
            for ref in (au, ad, sum_ref, up_ref):
                ref[...] = jnp.zeros_like(ref)

        hat, _ = normalized(x_ref[...].astype(F32))
        one = (hat * norm_ref[0:1] + norm_ref[1:2]).astype(BF)
        two = (hat * norm_ref[2:3] + norm_ref[3:4]).astype(BF)
        cot = cot_ref[...]
        proj_ref[...] = nn(one, w_qkv) + bq_ref[...]
        mixed_ref[...] = nt(cot, wo_ref[...]).astype(BF)
        pre = nn(two, w_up) + bu_ref[...]
        bell = half_erf(pre)
        hidden = (pre * bell).astype(BF)
        out_ref[...] = nn(hidden, w_down).astype(BF)
        slope = bell + pre * jnp.exp(-0.5 * pre * pre) * (1.0 / math.sqrt(2.0 * math.pi))
        grad_pre = (nt(cot, w_down) * slope).astype(BF)
        arriving = nt(grad_pre, w_up)
        q_ref[...] = (arriving * norm_ref[2:3]).astype(BF)
        sum_ref[0] += rows8(arriving * hat)
        sum_ref[1] += rows8(arriving)
        up_ref[...] += rows8(grad_pre.astype(F32))
        ad[...] += tn(hidden, cot)
        au[...] += tn(two, grad_pre)

        @pl.when(step == last)
        def _():
            spread_out(all_ref, (ad, au), nf)

    ins = (toks, cots, norms, weights, b_qkv, w_out, b_up)
    return pl.pallas_call(
        kernel,
        grid_spec=pltpu.PrefetchScalarGridSpec(
            num_scalar_prefetch=1,
            grid=(n, c // BLK),
            in_specs=[tokens_spec(d)] * 2 + [whole_spec(a.shape) for a in ins[2:]],
            out_specs=(
                tokens_spec(wide), tokens_spec(width),
                pl.BlockSpec((None, BLK, d), lambda i, j, r: (lax.rem(r[0] - i + n, n), j, 0)),
                tokens_spec(d),
                whole_spec((nf, tall, d)), whole_spec((2, 8, d)), whole_spec((8, hid)),
            ),
            scratch_shapes=[pltpu.VMEM((d, hid), F32), pltpu.VMEM((hid, d), F32)],
        ),
        out_shape=(
            jax.ShapeDtypeStruct((n, c, wide), F32),
            jax.ShapeDtypeStruct((n, c, width), BF),
            jax.ShapeDtypeStruct((n, c, d), BF),
            jax.ShapeDtypeStruct((n, c, d), BF),
            jax.ShapeDtypeStruct((nf, tall, d), BF),
            jax.ShapeDtypeStruct((2, 8, d), F32),
            jax.ShapeDtypeStruct((8, hid), F32),
        ),
        compiler_params=pltpu.CompilerParams(vmem_limit_bytes=60 << 20),
        cost_estimate=pl.CostEstimate(
            flops=2 * n * c * d * (wide + width + 6 * hid), bytes_accessed=30 << 20,
            transcendentals=2 * n * c * hid,
        ),
        name="feed",
    )(rank, *ins)


def finish(nf, tall, toks, cots, rest, grad_proj, mixed, norms, weights):
    n, c, d = toks.shape
    wide, width = grad_proj.shape[2], mixed.shape[2]
    last = n * (c // BLK) - 1

    def kernel(
        x_ref, cot_ref, rest_ref, gp_ref, mixed_ref, norm_ref, wq_ref,
        q_ref, all_ref, sum_ref, aq, ao,
    ):
        step = pl.program_id(0) * (c // BLK) + pl.program_id(1)

        @pl.when(step == 0)
        def _():
            for ref in (aq, ao, sum_ref):
                ref[...] = jnp.zeros_like(ref)

        hat, _ = normalized(x_ref[...].astype(F32))
        one = (hat * norm_ref[0:1] + norm_ref[1:2]).astype(BF)
        grad_proj = gp_ref[...]
        arriving = nt(grad_proj, wq_ref[:, wq_ref.shape[1] - wide :])
        q_ref[...] = (arriving * norm_ref[0:1] + rest_ref[...].astype(F32)).astype(BF)
        sum_ref[0] += rows8(arriving * hat)
        sum_ref[1] += rows8(arriving)
        aq[...] += tn(one, grad_proj)
        ao[...] += tn(mixed_ref[...], cot_ref[...])

        @pl.when(step == last)
        def _():
            spread_out(all_ref, (aq, ao), nf)

    ins = (toks, cots, rest, grad_proj, mixed, norms, weights)
    return pl.pallas_call(
        kernel,
        grid=(n, c // BLK),
        in_specs=[tokens_spec(a.shape[2]) for a in ins[:5]] + [whole_spec(a.shape) for a in ins[5:]],
        out_specs=(tokens_spec(d), whole_spec((nf, tall, d)), whole_spec((2, 8, d))),
        out_shape=(
            jax.ShapeDtypeStruct((n, c, d), BF),
            jax.ShapeDtypeStruct((nf, tall, d), BF),
            jax.ShapeDtypeStruct((2, 8, d), F32),
        ),
        scratch_shapes=[pltpu.VMEM((d, wide), F32), pltpu.VMEM((width, d), F32)],
        compiler_params=pltpu.CompilerParams(vmem_limit_bytes=60 << 20),
        cost_estimate=pl.CostEstimate(
            flops=n * c * d, bytes_accessed=n * c * d, transcendentals=0
        ),
        name="finish",
    )(*ins)


def make_body(nf, n):
    both = ("fsdp", "seq")

    def send(x, k):
        return lax.ppermute(x, "seq", [(i, (i + k) % n) for i in range(n)])

    def hop(x, pairs):
        return lax.ppermute(x, "seq", pairs)

    def gather_ring(x, rank, between):
        right, left = [x], [x]
        for t in range(1, n):
            right[-1], left[-1] = between(t, (right[-1], left[-1]))
            right.append(hop(right[-1], [(i, i + 1) for i in range(t - 1, n - 1)]))
            left.append(hop(left[-1], [(i, i - 1) for i in range(1, n - t + 1)]))
        return [x] + [jnp.where(rank >= k, right[k], left[n - k]) for k in range(1, n)]

    def scatter_ring(parts, between):
        right = left = None
        for t in range(1, n):
            if t == n - 1:
                between((right, left))
            rising = parts[t] if right is None else parts[t].astype(F32) + right.astype(F32)
            falling = parts[n - t] if left is None else parts[n - t].astype(F32) + left.astype(F32)
            right = hop(rising.astype(BF), [(i, i + 1) for i in range(t)])
            left = hop(falling.astype(BF), [(i, i - 1) for i in range(n - t, n)])
        return parts[0].astype(F32) + (right.astype(F32) + left.astype(F32))

    def in_order(parts, rank):
        out = jnp.zeros((n,) + parts[0].shape, parts[0].dtype)
        for k in range(n):
            out = lax.dynamic_update_index_in_dim(out, parts[k], (rank - k) % n, 0)
        return out

    def exchange(blocks, rank):
        own = [lax.dynamic_index_in_dim(blocks, (rank + k) % n, 0, keepdims=False) for k in range(n)]
        return in_order([send(own[k], k) if k else own[k] for k in range(n)], rank)

    def body(
        tokens,
        cotangent,
        w_qkv,
        b_qkv,
        w_out,
        b_out,
        w_up,
        b_up,
        w_down,
        b_down,
        gain_attn,
        shift_attn,
        gain_mlp,
        shift_mlp,
    ):
        rank = lax.axis_index("seq")
        _, c, d = tokens.shape
        rows = w_qkv.shape[0]
        width = d // n
        wide = 3 * width
        units = w_down.shape[0]
        extra = 8
        while n * (rows + extra) % 16:
            extra += 1
        tok = tokens.reshape(c, d)
        cot = cotangent.reshape(c, d)

        vectors = (b_qkv, b_out, b_up, b_down, gain_attn, shift_attn, gain_mlp, shift_mlp)
        lengths = [v.shape[0] for v in vectors]
        total = sum(lengths)
        pack = jnp.stack([jnp.pad(v, (0, d - v.shape[0])) for v in vectors])
        same = jnp.concatenate([w_out, pack, jnp.zeros((extra - len(vectors), d), BF)])
        qkv_cols = w_qkv.reshape(rows, 3, n, width).transpose(2, 0, 1, 3).reshape(n, rows, wide)
        up_cols = w_up.reshape(rows, nf, n, units).transpose(2, 0, 1, 3).reshape(n, rows, nf * units)
        message = jnp.concatenate(
            [
                jnp.broadcast_to(same, (n, rows + extra, d)),
                jnp.pad(up_cols, ((0, 0), (0, extra), (0, 0))),
                jnp.pad(qkv_cols, ((0, 0), (0, extra), (0, 0))),
            ],
            axis=2,
        )
        found = []

        def prepare():
            blocks = found[0].reshape(nf, n, rows + extra, d)
            full_out = blocks[:, :, :rows].reshape(d, d)
            full = [
                blocks[:, :, rows + i, :size].reshape(-1).astype(F32)
                for i, size in enumerate(lengths)
            ]
            norms = jnp.stack(full[4:] + [jnp.zeros((d,), F32)] * 4)
            own_bias_qkv = lax.dynamic_index_in_dim(full[0].reshape(3, n, width), rank, 1)
            own_bias_up = lax.dynamic_index_in_dim(full[2].reshape(nf, n, units), rank, 1)
            out_blocks = [
                lax.dynamic_slice_in_dim(full_out, (rank + k) % n * width, width, 0) for k in range(n)
            ]
            return (
                full[1] + full[3], norms, own_bias_qkv.reshape(1, -1), own_bias_up.reshape(1, -1),
                out_blocks,
            )

        def between(t, passed):
            if t == 2:
                tables = [
                    rot_tables((rank - k) % n * c + jnp.arange(c, dtype=jnp.int32)) for k in range(n)
                ]
                tables = [jnp.stack(t) for t in zip(*tables)]
                mine, tables, passed = lax.optimization_barrier((message, tables, passed))
                mine = exchange(mine, rank)
                head = mine[:, :, :d].reshape(n * (rows + extra), d)
                found.append(lax.all_gather(head, "fsdp", axis=0, tiled=True))
                side = mine[:, :rows, d:].reshape(n * rows, -1)
                hid = nf * units
                side = jnp.concatenate([side[:, :hid], w_down, side[:, hid:]], axis=1)
                found.append(lax.all_gather(side, "fsdp", axis=0, tiled=True))
                found.append(tables)
            return passed

        chunks = gather_ring(jnp.stack([tok, cot]), rank, between)
        toks = jnp.stack([pair[0] for pair in chunks])
        cots = jnp.stack([pair[1] for pair in chunks])
        _, weights, tables = found
        bias_ends, norms, own_bias_qkv, own_bias_up, out_blocks = prepare()

        def packed_row(sums, sizes):
            row = jnp.concatenate([v.reshape(nf, n, size) for v, size in zip(sums, sizes)], axis=2)
            row = row.reshape(nf, 1, n * sum(sizes)).astype(BF)
            return jnp.pad(row, ((0, 0), (0, 0), (0, d - row.shape[2])))

        def place(values, parts):
            mine = lax.broadcasted_iota(jnp.int32, (1, n, 1), 1) == rank
            return jnp.where(mine, values.reshape(parts, 1, -1), 0.0).reshape(-1)

        cot_float = cot.astype(F32)
        sum_out = jnp.sum(cot_float, axis=0)
        projected, grad_mixed, mlp_parts, rest, joined, sums_two, sum_up = feed(
            nf, -(-(2 * units + 1) // 16) * 16 - 2 * units,
            jnp.full((1,), rank, jnp.int32), toks, cots, norms, weights,
            own_bias_qkv, out_blocks[0], own_bias_up,
        )
        mlp_out = lax.psum_scatter(
            mlp_parts.reshape(n * c, d), "seq", scatter_dimension=0, tiled=True
        )
        sums_two = jnp.sum(sums_two, axis=1)
        sizes = (lengths[1], lengths[2], lengths[3], lengths[6], lengths[7])
        row = packed_row(
            (sum_out, place(jnp.sum(sum_up, axis=0), nf), sum_out, sums_two[0], sums_two[1]), sizes
        )
        joined = lax.dynamic_update_slice(joined, row, (0, 2 * units, 0))
        joined = lax.all_to_all(joined, "fsdp", split_axis=0, concat_axis=0, tiled=True)
        mixed, grad_proj, sum_qkv = attend(
            jnp.full((1,), rank, jnp.int32), projected, grad_mixed, tables
        )
        mlp_out, joined, mixed, grad_proj = lax.optimization_barrier(
            (mlp_out, joined, mixed, grad_proj)
        )
        mixed_own = [send(mixed[k], -k) if k else mixed[k] for k in range(n)]
        filled = n * rows + rows
        tall = -(-(filled + 1) // 16) * 16
        grad_q, tail, sums_one = finish(
            nf, tall, toks, cots, rest, grad_proj, mixed, norms, weights
        )
        mixed_own, grad_q = lax.optimization_barrier((mixed_own, grad_q))

        sums_one = jnp.sum(sums_one, axis=1)
        late = (lengths[0], lengths[4], lengths[5])
        row = packed_row((place(jnp.sum(sum_qkv, axis=0), 3), sums_one[0], sums_one[1]), late)
        tail = lax.dynamic_update_slice(tail, row, (0, filled, 0))
        tail = lax.psum_scatter(tail.reshape(-1, d), "fsdp", scatter_dimension=0, tiled=True)
        joined = jnp.sum(joined.astype(F32), axis=0)
        grad_w_down = joined[:units]
        joined = joined[units:].astype(BF)
        grad_w_out = lax.ppermute(
            tail[n * rows : filled],
            both,
            [(f * n + s, s * nf + f) for f in range(nf) for s in range(n)],
        ).astype(F32)

        def to_owners(block, line, sizes):
            line = line[0, : n * sum(sizes)].reshape(n, 1, sum(sizes))
            line = jnp.pad(line, ((0, 0), (0, 0), (0, d - sum(sizes))))
            block = jnp.concatenate([block.reshape(n, rows, d), line], axis=1)
            block = exchange(block, rank).astype(F32)
            line = jnp.sum(block[:, rows], axis=0)
            parts = []
            at = 0
            for size in sizes:
                parts.append(line[at : at + size])
                at += size
            return block[:, :rows], parts

        grad_up, early_sums = to_owners(
            joined[:units], joined[units : units + 1], sizes
        )
        grad_w_up = grad_up.reshape(n, rows, nf, units).transpose(1, 2, 0, 3).reshape(rows, -1)
        grad_qkv, late_sums = to_owners(tail[: n * rows], tail[filled : filled + 1], late)
        grad_w_qkv = (
            grad_qkv[:, :, :wide].reshape(n, rows, 3, width).transpose(1, 2, 0, 3).reshape(rows, -1)
        )
        grads = [late_sums[0]] + early_sums[:3] + late_sums[1:] + early_sums[3:]

        x = tok.astype(F32)
        held = []

        def between(passed):
            mixed_here, _ = lax.optimization_barrier((mixed_own, passed))
            out = x + bias_ends + mlp_out.astype(F32)
            for k in range(n):
                out = out + nn(mixed_here[k], out_blocks[k])
            held.append(out)

        grad_q = scatter_ring([grad_q[k] for k in range(n)], between)
        block_out = held[0]
        hat, spread = normalized(x)
        grad_tokens = cot_float + spread * (
            grad_q
            - jnp.mean(grad_q, axis=-1, keepdims=True)
            - hat * jnp.mean(grad_q * hat, axis=-1, keepdims=True)
        )

        return (
            block_out.astype(BF).reshape(tokens.shape),
            grad_tokens.astype(BF).reshape(tokens.shape),
            grad_w_qkv,
            grads[0],
            grad_w_out,
            grads[1],
            grad_w_up,
            grads[2],
            grad_w_down,
            grads[3],
            grads[4],
            grads[5],
            grads[6],
            grads[7],
        )

    return body


def solution(mesh):
    tok = P("fsdp", "seq", None)
    mat = P(("fsdp", "seq"), None)
    vec = P(("fsdp", "seq"))
    params = (mat, vec, mat, vec, mat, vec, mat, vec, vec, vec, vec, vec)
    return jax.shard_map(
        make_body(mesh.shape["fsdp"], mesh.shape["seq"]),
        mesh=mesh,
        in_specs=(tok, tok) + params,
        out_specs=(tok, tok) + params,
        check_vma=False,
    )
```

profile of v0, /device:TPU:0, one launch (start us, length us, event | category | flops | bytes accessed | tf_op | source)
XLA Modules:
  0.0 368.7 jit_solution(10623939294139874775)
XLA Ops:
  7.2 2.1 constant_dynamic-update-slice_fusion.1
  9.5 1.6 fusion.76
  11.1 5.0 %collective-permute-start = (bf16[2,512,768]{2,1,0:T(8,128)(2,1)}, bf16[2,512,768]{2,1,0:T(8,128)(2,1)S(1)}, u32[]{:S(2)}, u32[]{:S(2)}) collective-permute-start(bf16[2,512,768]{2,1,0:T(8,128)(2,1)} %get-tuple-element.106), channel_id=1, source_target_pairs={{0,1},{1,2},{2,3},{4,5},{5,6},{6,7},{8,9},{9,10},{10,11},{12,13},{... | collective-permute-start | bytes 4718600 | tf_op jit(solution)/shard_map/ppermute | solution.py:338
  16.1 1.3 collective-permute-start.1
  18.8 3.8 %fusion.35 = (f32[1,512,128]{2,1,0:T(8,128)S(1)}, f32[1,512,128]{2,1,0:T(8,128)S(1)}, f32[1,512,128]{2,1,0:T(8,128)S(1)}, f32[1,512,128]{2,1,0:T(8,128)S(1)}, f3...) fusion(f32[512]{0:T(512)S(1)} %get-tuple-element.148, ...), kind=kLoop, calls=%fused_computation.66 | loop fusion | flops 1310720 | bytes 3154816 | tf_op jit(solution)/shard_map/jit(_where)/select_n | solution.py:27
  22.7 1.0 pad_maximum_fusion.2.c_ref
  23.7 1.1 pad_maximum_fusion.3.sa_ref
  24.8 1.1 pad_maximum_fusion.4.sb_ref
  25.9 24.0 %collective-permute-done = bf16[2,512,768]{2,1,0:T(8,128)(2,1)S(1)} collective-permute-done((bf16[2,512,768]{2,1,0:T(8,128)(2,1)}, bf16[2,512,768]{2,1,0:T(8,128)(2,1)S(1)}, u32[]{:S(2)}, u32[]{:S(2)}) %collective-permute-start) | collective-permute-done | bytes 1572896 | tf_op jit(solution)/shard_map/ppermute | solution.py:338
  50.0 4.2 %collective-permute-done.1 = bf16[2,512,768]{2,1,0:T(8,128)(2,1)} collective-permute-done((bf16[2,512,768]{2,1,0:T(8,128)(2,1)}, bf16[2,512,768]{2,1,0:T(8,128)(2,1)}, u32[]{:S(2)}, u32[]{:S(2)}) %collective-permute-start.1) | collective-permute-done | bytes 1572896 | tf_op jit(solution)/shard_map/ppermute | solution.py:338
  54.9 1.5 collective-permute-start.2
  56.4 1.0 collective-permute-start.3
  57.4 2.9 collective-permute-start.4
  60.4 3.4 collective-permute-done.2
  64.6 2.6 collective-permute-done.3
  69.1 1.8 collective-permute-start.7
  70.9 1.3 collective-permute-start.5
  72.2 1.9 collective-permute-start.8
  74.1 37.6 %collective-permute-done.5 = bf16[2,512,768]{2,1,0:T(8,128)(2,1)} collective-permute-done((bf16[2,512,768]{2,1,0:T(8,128)(2,1)}, bf16[2,512,768]{2,1,0:T(8,128)(2,1)}, u32[]{:S(2)}, u32[]{:S(2)}) %collective-permute-start.5) | collective-permute-done | bytes 1572896 | tf_op jit(solution)/shard_map/ppermute | solution.py:338
  111.7 1.5 collective-permute-start.6
  113.2 1.6 broadcast_select_fusion.1
  115.7 1.4 slice.225
  118.0 1.7 fusion.62
  123.9 1.6 broadcast_select_fusion
  125.7 23.1 %collective-permute-done.6 = bf16[2,512,768]{2,1,0:T(8,128)(2,1)} collective-permute-done((bf16[2,512,768]{2,1,0:T(8,128)(2,1)}, bf16[2,512,768]{2,1,0:T(8,128)(2,1)}, u32[]{:S(2)}, u32[]{:S(2)}) %collective-permute-start.6) | collective-permute-done | bytes 1572896 | tf_op jit(solution)/shard_map/ppermute | solution.py:338
  148.7 1.6 broadcast_select_fusion.2
  150.5 1.0 copy-done
  151.7 1.9 pad_maximum_fusion.x_ref
  153.6 1.9 pad_maximum_fusion.1.cot_ref
  155.6 29.8 %feed.1 = (f32[4,512,576]{2,1,0:T(8,128)}, bf16[4,512,192]{2,1,0:T(8,128)(2,1)}, bf16[4,512,768]{2,1,0:T(8,128)(2,1)}, bf16[4,512,768]{2,1,0:T(8,128)(2,1)}, bf1...) custom-call(s32[1]{0:T(128)} %bitcast.11.rank_ref, bf16[4,512,768]{2,1,0:T(8,128)(2,1)} %pad_maximum_fusion.x_ref, ...), custom_call_target="tpu_custom_call" | custom-call | flops 16911433728 | bytes 31457280 | tf_op jit(solution)/shard_map/feed/pallas_call | solution.py:249
  186.9 1.6 dynamic_update_slice.48
  188.5 3.7 %all-to-all-start = ((bf16[8,208,768]{2,1,0:T(8,128)(2,1)}), bf16[8,208,768]{2,1,0:T(8,128)(2,1)S(1)}, u32[]{:S(2)}, u32[]{:S(2)}) async-start(bf16[8,208,768]{2,1,0:T(8,128)(2,1)} %dynamic_update_slice.48), calls=%async_computation.1 | async-start | bytes 5111808 | tf_op jit(solution)/shard_map/all_to_all | solution.py:480
  194.1 44.1 %attend.1 = (bf16[4,512,192]{2,1,0:T(8,128)(2,1)}, bf16[4,512,576]{2,1,0:T(8,128)(2,1)}, f32[8,576]{1,0:T(8,128)}) custom-call(s32[1]{0:T(128)} %bitcast.11.rank_ref, f32[4,512,576]{2,1,0:T(8,128)} %get-tuple-element.53.proj_ref, bf16[4,512,192]{2,1,0:T(8,128)(2,1)} %get-tuple-element.54.gm_ref, f32[4,512,128]{2,1,0:T(8,128)} %pad_maximum_fusion.2.c_ref, ...), custom_call_target="tpu_custom_call" | custom-call | flops 4831838208 | bytes 16777216 | tf_op jit(solution)/shard_map/attend/pallas_call | solution.py:146
  239.2 4.9 %reduce-scatter.3.cloned.1.call-done = bf16[512,768]{1,0:T(8,128)(2,1)} async-done(((bf16[2048,768]{1,0:T(8,128)(2,1)}), bf16[512,768]{1,0:T(8,128)(2,1)}) %reduce-scatter.3.cloned.1.call-update) | async-done | bytes 786448 | tf_op jit(solution)/shard_map/reduce_scatter | solution.py:471
  244.1 2.2 slice_bitcast_fusion.2
  246.3 2.0 collective-permute-start.9
  248.7 2.0 collective-permute-start.11
  250.7 14.3 %finish.1 = (bf16[4,512,768]{2,1,0:T(8,128)(2,1)}, bf16[8,128,768]{2,1,0:T(8,128)(2,1)}, f32[2,8,768]{2,1,0:T(8,128)}) custom-call(bf16[4,512,768]{2,1,0:T(8,128)(2,1)} %pad_maximum_fusion.x_ref, bf16[4,512,768]{2,1,0:T(8,128)(2,1)} %pad_maximum_fusion.1.cot_ref, bf16[4,512,768]{2,1,0:T(8,128)(2,1)} %get-tuple-element.62.rest_ref, ...), custom_call_target="tpu_custom_call" | custom-call | flops 1572864 | bytes 1572864 | tf_op jit(solution)/shard_map/finish/pallas_call | solution.py:312
  265.8 1.2 convert_reduce_fusion
  267.0 5.1 %collective-permute-done.10 = bf16[512,192]{1,0:T(8,128)(2,1)} collective-permute-done((bf16[512,192]{1,0:T(8,128)(2,1)}, bf16[512,192]{1,0:T(8,128)(2,1)}, u32[]{:S(2)}, u32[]{:S(2)}) %collective-permute-start.10) | collective-permute-done | bytes 196640 | tf_op jit(solution)/shard_map/ppermute | solution.py:335
  272.3 1.7 collective-permute-start.14
  274.0 3.4 collective-permute-start.12
  278.9 1.6 dynamic_update_slice.49
  280.5 4.0 %collective-permute-start.23 = (bf16[25,768]{1,0:T(8,128)(2,1)S(1)}, bf16[25,768]{1,0:T(8,128)(2,1)S(1)}, u32[]{:S(2)}, u32[]{:S(2)}) collective-permute-start(bf16[25,768]{1,0:T(8,128)(2,1)S(1)} %get-tuple-element.112), channel_id=1, source_target_pairs={{0,2},{1,3},{2,0},{3,1},{4,6},{5,7},{6,4},{7,5},{8,10},{9,11},{10,... | collective-permute-start | bytes 115208 | tf_op jit(solution)/shard_map/ppermute | solution.py:335
  284.5 13.2 %collective-permute-done.22 = bf16[25,768]{1,0:T(8,128)(2,1)S(1)} collective-permute-done((bf16[25,768]{1,0:T(8,128)(2,1)S(1)}, bf16[25,768]{1,0:T(8,128)(2,1)S(1)}, u32[]{:S(2)}, u32[]{:S(2)}) %collective-permute-start.22) | collective-permute-done | bytes 38432 | tf_op jit(solution)/shard_map/ppermute | solution.py:335
  297.8 3.1 fusion.19
  300.9 3.0 collective-permute-start.13
  303.8 1.5 collective-permute-start.15
  306.0 1.1 reshape.1138
  308.2 10.4 %collective-permute-done.13 = bf16[512,768]{1,0:T(8,128)(2,1)} collective-permute-done((bf16[512,768]{1,0:T(8,128)(2,1)}, bf16[512,768]{1,0:T(8,128)(2,1)}, u32[]{:S(2)}, u32[]{:S(2)}) %collective-permute-start.13) | collective-permute-done | bytes 786464 | tf_op jit(solution)/shard_map/ppermute | solution.py:338
  318.6 3.4 add_convert_fusion.1
  322.0 1.3 collective-permute-start.17
  323.3 7.8 %collective-permute-start.16 = (bf16[512,768]{1,0:T(8,128)(2,1)}, bf16[512,768]{1,0:T(8,128)(2,1)}, u32[]{:S(2)}, u32[]{:S(2)}) collective-permute-start(bf16[512,768]{1,0:T(8,128)(2,1)} %get-tuple-element.89), channel_id=1, source_target_pairs={{0,1},{1,2},{2,3},{4,5},{5,6},{6,7},{8,9},{9,10},{10,11},{12,13},{... | collective-permute-start | bytes 2359304 | tf_op jit(solution)/shard_map/ppermute | solution.py:338
  331.1 1.3 fusion.41
  332.4 2.5 fusion.43
  335.0 1.5 fusion.79
  337.3 1.0 slice.231
  338.4 1.2 collective-permute-start.18
  341.0 3.4 fusion.23
  344.4 5.2 %collective-permute-start.19 = (bf16[25,768]{1,0:T(8,128)(2,1)S(1)}, bf16[25,768]{1,0:T(8,128)(2,1)S(1)}, u32[]{:S(2)}, u32[]{:S(2)}) collective-permute-start(bf16[25,768]{1,0:T(8,128)(2,1)S(1)} %get-tuple-element.116), channel_id=1, source_target_pairs={{0,2},{1,3},{2,0},{3,1},{4,6},{5,7},{6,4},{7,5},{8,10},{9,11},{10,... | collective-permute-start | bytes 115208 | tf_op jit(solution)/shard_map/ppermute | solution.py:335
  349.6 1.9 collective-permute-start.20
  352.3 1.7 collective-permute-done.20
  356.5 2.4 fusion.53
  358.9 3.3 fusion.24
  (217 shorter events, 25.3 us)
Async XLA Ops:
  7.2 2.2 copy-start.2
  7.2 10.3 %copy-start.15 = (bf16[24,2304]{1,0:T(8,128)(2,1)S(1)}, bf16[24,2304]{1,0:T(8,128)(2,1)}, u32[]{:S(2)}) copy-start(bf16[24,2304]{1,0:T(8,128)(2,1)} %param.16) | copy-start | bytes 331780
  7.2 108.5 %all-gather.3.cloned.1.call-start = ((), (), s32[]{:S(2)}) async-start(), calls=%async_computation.3 | async-start | bytes 1769472 | tf_op jit(solution)/shard_map/all_gather | solution.py:441
  9.4 8.6 %copy-start.14 = (bf16[24,3072]{1,0:T(8,128)(2,1)S(1)}, bf16[24,3072]{1,0:T(8,128)(2,1)}, u32[]{:S(2)}) copy-start(bf16[24,3072]{1,0:T(8,128)(2,1)} %param.20) | copy-start | bytes 442372
  9.4 9.0 %copy-start.24 = (bf16[72]{0:T(256)(128)(2,1)S(1)}, bf16[72]{0:T(256)(128)(2,1)}, u32[]{:S(2)}) copy-start(bf16[72]{0:T(256)(128)(2,1)} %param.17) | copy-start | bytes 436
  9.4 9.0 %copy-start.25 = (bf16[24]{0:T(256)(128)(2,1)S(1)}, bf16[24]{0:T(256)(128)(2,1)}, u32[]{:S(2)}) copy-start(bf16[24]{0:T(256)(128)(2,1)} %param.19) | copy-start | bytes 148
  9.4 9.0 %copy-start.26 = (bf16[96]{0:T(256)(128)(2,1)S(1)}, bf16[96]{0:T(256)(128)(2,1)}, u32[]{:S(2)}) copy-start(bf16[96]{0:T(256)(128)(2,1)} %param.21) | copy-start | bytes 580
  9.4 9.1 %copy-start.27 = (bf16[24]{0:T(256)(128)(2,1)S(1)}, bf16[24]{0:T(256)(128)(2,1)}, u32[]{:S(2)}) copy-start(bf16[24]{0:T(256)(128)(2,1)} %param.23) | copy-start | bytes 148
  9.4 9.1 %copy-start.28 = (bf16[24]{0:T(256)(128)(2,1)S(1)}, bf16[24]{0:T(256)(128)(2,1)}, u32[]{:S(2)}) copy-start(bf16[24]{0:T(256)(128)(2,1)} %param.24) | copy-start | bytes 148
  9.4 9.1 %copy-start.29 = (bf16[24]{0:T(256)(128)(2,1)S(1)}, bf16[24]{0:T(256)(128)(2,1)}, u32[]{:S(2)}) copy-start(bf16[24]{0:T(256)(128)(2,1)} %param.25) | copy-start | bytes 148
  9.5 9.1 %copy-start.30 = (bf16[24]{0:T(256)(128)(2,1)S(1)}, bf16[24]{0:T(256)(128)(2,1)}, u32[]{:S(2)}) copy-start(bf16[24]{0:T(256)(128)(2,1)} %param.26) | copy-start | bytes 148
  9.5 9.1 %copy-start.31 = (bf16[24]{0:T(256)(128)(2,1)S(1)}, bf16[24]{0:T(256)(128)(2,1)}, u32[]{:S(2)}) copy-start(bf16[24]{0:T(256)(128)(2,1)} %param.27) | copy-start | bytes 148
  9.5 9.2 %copy-start.17 = (bf16[24,768]{1,0:T(8,128)(2,1)S(1)}, bf16[24,768]{1,0:T(8,128)(2,1)}, u32[]{:S(2)}) copy-start(bf16[24,768]{1,0:T(8,128)(2,1)} %param.18) | copy-start | bytes 110596
  11.1 38.9 %collective-permute-start = (bf16[2,512,768]{2,1,0:T(8,128)(2,1)}, bf16[2,512,768]{2,1,0:T(8,128)(2,1)S(1)}, u32[]{:S(2)}, u32[]{:S(2)}) collective-permute-start(bf16[2,512,768]{2,1,0:T(8,128)(2,1)} %get-tuple-element.106), channel_id=1, source_target_pairs={{0,1},{1,2},{2,3},{4,5},{5,6},{6,7},{8,9},{9,10},{10,11},{12,13},{... | collective-permute-start | bytes 4718600 | tf_op jit(solution)/shard_map/ppermute | solution.py:338
  16.1 38.1 %collective-permute-start.1 = (bf16[2,512,768]{2,1,0:T(8,128)(2,1)}, bf16[2,512,768]{2,1,0:T(8,128)(2,1)}, u32[]{:S(2)}, u32[]{:S(2)}) collective-permute-start(bf16[2,512,768]{2,1,0:T(8,128)(2,1)} %get-tuple-element.106), channel_id=1, source_target_pairs={{1,0},{2,1},{3,2},{5,4},{6,5},{7,6},{9,8},{10,9},{11,10},{13,12},{... | collective-permute-start | bytes 4718600 | tf_op jit(solution)/shard_map/ppermute | solution.py:338
  50.0 19.1 %copy-start.8 = (bf16[2,512,768]{2,1,0:T(8,128)(2,1)}, bf16[2,512,768]{2,1,0:T(8,128)(2,1)S(1)}, u32[]{:S(2)}) copy-start(bf16[2,512,768]{2,1,0:T(8,128)(2,1)S(1)} %collective-permute-done) | copy-start | bytes 4718596
  54.2 14.0 %copy-start.13 = (bf16[96,768]{1,0:T(8,128)(2,1)S(1)}, bf16[96,768]{1,0:T(8,128)(2,1)}, u32[]{:S(2)}) copy-start(bf16[96,768]{1,0:T(8,128)(2,1)} %param.22) | copy-start | bytes 442372
  54.9 8.8 %collective-permute-start.2 = (bf16[32,2112]{1,0:T(8,128)(2,1)}, bf16[32,2112]{1,0:T(8,128)(2,1)}, u32[]{:S(2)}, u32[]{:S(2)}) collective-permute-start(bf16[32,2112]{1,0:T(8,128)(2,1)} %get-tuple-element.109), channel_id=1, source_target_pairs={{0,1},{1,2},{2,3},{3,0},{4,5},{5,6},{6,7},{7,4},{8,9},{9,10},{10,1... | collective-permute-start | bytes 405512 | tf_op jit(solution)/shard_map/ppermute | solution.py:335
  56.4 10.9 %collective-permute-start.3 = (bf16[32,2112]{1,0:T(8,128)(2,1)S(1)}, bf16[32,2112]{1,0:T(8,128)(2,1)S(1)}, u32[]{:S(2)}, u32[]{:S(2)}) collective-permute-start(bf16[32,2112]{1,0:T(8,128)(2,1)S(1)} %get-tuple-element.108), channel_id=1, source_target_pairs={{0,2},{1,3},{2,0},{3,1},{4,6},{5,7},{6,4},{7,5},{8,10},{9,11},{10,... | collective-permute-start | bytes 405512 | tf_op jit(solution)/shard_map/ppermute | solution.py:335
  57.4 9.9 %collective-permute-start.4 = (bf16[32,2112]{1,0:T(8,128)(2,1)S(1)}, bf16[32,2112]{1,0:T(8,128)(2,1)S(1)}, u32[]{:S(2)}, u32[]{:S(2)}) collective-permute-start(bf16[32,2112]{1,0:T(8,128)(2,1)S(1)} %get-tuple-element.107), channel_id=1, source_target_pairs={{0,3},{1,0},{2,1},{3,2},{4,7},{5,4},{6,5},{7,6},{8,11},{9,8},{10,9... | collective-permute-start | bytes 405512 | tf_op jit(solution)/shard_map/ppermute | solution.py:335
  68.1 87.5 %all-gather.5.cloned.1.call-start = ((), (), s32[]{:S(2)}) async-start(), calls=%async_computation.4 | async-start | bytes 3760128 | tf_op jit(solution)/shard_map/all_gather | solution.py:445
  69.0 175.1 %reduce-scatter.3.cloned.1.call-start = ((), (), s32[]{:S(2)}) async-start(), calls=%async_computation.5 | async-start | bytes 3932160 | tf_op jit(solution)/shard_map/reduce_scatter | solution.py:471
  69.1 3.1 collective-permute-start.7
  70.9 40.8 %collective-permute-start.5 = (bf16[2,512,768]{2,1,0:T(8,128)(2,1)}, bf16[2,512,768]{2,1,0:T(8,128)(2,1)}, u32[]{:S(2)}, u32[]{:S(2)}) collective-permute-start(bf16[2,512,768]{2,1,0:T(8,128)(2,1)} %collective-permute-done.1), channel_id=1, source_target_pairs={{1,0},{2,1},{5,4},{6,5},{9,8},{10,9},{13,12},{14,13},{17,16},{18,1... | collective-permute-start | bytes 4718600 | tf_op jit(solution)/shard_map/ppermute | solution.py:338
  72.2 51.8 %collective-permute-start.8 = (bf16[2,512,768]{2,1,0:T(8,128)(2,1)}, bf16[2,512,768]{2,1,0:T(8,128)(2,1)}, u32[]{:S(2)}, u32[]{:S(2)}) collective-permute-start(bf16[2,512,768]{2,1,0:T(8,128)(2,1)} %collective-permute-done.7), channel_id=1, source_target_pairs={{2,3},{6,7},{10,11},{14,15},{18,19},{22,23},{26,27},{30,31}} | collective-permute-start | bytes 4718600 | tf_op jit(solution)/shard_map/ppermute | solution.py:338
  111.7 37.0 %collective-permute-start.6 = (bf16[2,512,768]{2,1,0:T(8,128)(2,1)}, bf16[2,512,768]{2,1,0:T(8,128)(2,1)}, u32[]{:S(2)}, u32[]{:S(2)}) collective-permute-start(bf16[2,512,768]{2,1,0:T(8,128)(2,1)} %collective-permute-done.5), channel_id=1, source_target_pairs={{1,0},{5,4},{9,8},{13,12},{17,16},{21,20},{25,24},{29,28}} | collective-permute-start | bytes 4718600 | tf_op jit(solution)/shard_map/ppermute | solution.py:338
  117.1 8.4 %copy-start.4 = (bf16[8,4,24,768]{3,2,1,0:T(8,128)(2,1)}, bf16[8,4,24,768]{3,2,1,0:T(8,128)(2,1)S(1)}, u32[]{:S(2)}) copy-start(bf16[8,4,24,768]{3,2,1,0:T(8,128)(2,1)S(1)} %slice.225) | copy-start | bytes 3538948
  125.5 23.2 %copy-start.9 = (bf16[2,512,768]{2,1,0:T(8,128)(2,1)S(1)}, bf16[2,512,768]{2,1,0:T(8,128)(2,1)}, u32[]{:S(2)}) copy-start(bf16[2,512,768]{2,1,0:T(8,128)(2,1)} %copy-done.8) | copy-start | bytes 4718596
  150.3 1.1 copy-start
  150.3 1.4 copy-start.7
  185.4 0.7 copy-start.23
  185.4 0.8 copy-start.20
  185.4 0.9 copy-start.16
  188.5 50.7 %all-to-all-start = ((bf16[8,208,768]{2,1,0:T(8,128)(2,1)}), bf16[8,208,768]{2,1,0:T(8,128)(2,1)S(1)}, u32[]{:S(2)}, u32[]{:S(2)}) async-start(bf16[8,208,768]{2,1,0:T(8,128)(2,1)} %dynamic_update_slice.48), calls=%async_computation.1 | async-start | bytes 5111808 | tf_op jit(solution)/shard_map/all_to_all | solution.py:480
  192.2 144.3 %reduce-scatter.5.cloned.1.call-start = ((), (), s32[]{:S(2)}) async-start(), calls=%async_computation.6 | async-start | bytes 1769472 | tf_op jit(solution)/shard_map/reduce_scatter | solution.py:499
  192.5 45.7 %copy-start.18 = (f32[512]{0:T(512)}, f32[512]{0:T(512)S(1)}, u32[]{:S(2)}) copy-start(f32[512]{0:T(512)S(1)} %broadcast_multiply_fusion.2) | copy-start | bytes 6148
  246.3 20.7 %collective-permute-start.9 = (bf16[512,192]{1,0:T(8,128)(2,1)}, bf16[512,192]{1,0:T(8,128)(2,1)}, u32[]{:S(2)}, u32[]{:S(2)}) collective-permute-start(bf16[512,192]{1,0:T(8,128)(2,1)} %get-tuple-element.103), channel_id=1, source_target_pairs={{0,3},{1,0},{2,1},{3,2},{4,7},{5,4},{6,5},{7,6},{8,11},{9,8},{10,9... | collective-permute-start | bytes 589832 | tf_op jit(solution)/shard_map/ppermute | solution.py:335
  248.3 23.8 %collective-permute-start.10 = (bf16[512,192]{1,0:T(8,128)(2,1)}, bf16[512,192]{1,0:T(8,128)(2,1)}, u32[]{:S(2)}, u32[]{:S(2)}) collective-permute-start(bf16[512,192]{1,0:T(8,128)(2,1)} %get-tuple-element.102), channel_id=1, source_target_pairs={{0,2},{1,3},{2,0},{3,1},{4,6},{5,7},{6,4},{7,5},{8,10},{9,11},{10,... | collective-permute-start | bytes 589832 | tf_op jit(solution)/shard_map/ppermute | solution.py:335
  248.7 23.5 %collective-permute-start.11 = (bf16[512,192]{1,0:T(8,128)(2,1)}, bf16[512,192]{1,0:T(8,128)(2,1)}, u32[]{:S(2)}, u32[]{:S(2)}) collective-permute-start(bf16[512,192]{1,0:T(8,128)(2,1)} %get-tuple-element.101), channel_id=1, source_target_pairs={{0,1},{1,2},{2,3},{3,0},{4,5},{5,6},{6,7},{7,4},{8,9},{9,10},{10,1... | collective-permute-start | bytes 589832 | tf_op jit(solution)/shard_map/ppermute | solution.py:335
  265.8 6.3 %copy-start.1 = (bf16[4,512,768]{2,1,0:T(8,128)(2,1)S(1)}, bf16[4,512,768]{2,1,0:T(8,128)(2,1)}, u32[]{:S(2)}) copy-start(bf16[4,512,768]{2,1,0:T(8,128)(2,1)} %get-tuple-element.69) | copy-start | bytes 9437188
  272.2 5.5 %copy-start.6 = (f32[208,768]{1,0:T(8,128)S(1)}, f32[208,768]{1,0:T(8,128)}, u32[]{:S(2)}) copy-start(f32[208,768]{1,0:T(8,128)} %convert_reduce_fusion) | copy-start | bytes 1916932
  272.3 25.5 %collective-permute-start.14 = (bf16[512,768]{1,0:T(8,128)(2,1)S(1)}, bf16[512,768]{1,0:T(8,128)(2,1)}, u32[]{:S(2)}, u32[]{:S(2)}) collective-permute-start(bf16[512,768]{1,0:T(8,128)(2,1)S(1)} %get-tuple-element.93), channel_id=1, source_target_pairs={{3,2},{7,6},{11,10},{15,14},{19,18},{23,22},{27,26},{31,30}} | collective-permute-start | bytes 2359304 | tf_op jit(solution)/shard_map/ppermute | solution.py:338
  274.0 23.8 %collective-permute-start.12 = (bf16[512,768]{1,0:T(8,128)(2,1)S(1)}, bf16[512,768]{1,0:T(8,128)(2,1)}, u32[]{:S(2)}, u32[]{:S(2)}) collective-permute-start(bf16[512,768]{1,0:T(8,128)(2,1)S(1)} %get-tuple-element.94), channel_id=1, source_target_pairs={{0,1},{4,5},{8,9},{12,13},{16,17},{20,21},{24,25},{28,29}} | collective-permute-start | bytes 2359304 | tf_op jit(solution)/shard_map/ppermute | solution.py:338
  277.9 19.9 %collective-permute-start.22 = (bf16[25,768]{1,0:T(8,128)(2,1)S(1)}, bf16[25,768]{1,0:T(8,128)(2,1)S(1)}, u32[]{:S(2)}, u32[]{:S(2)}) collective-permute-start(bf16[25,768]{1,0:T(8,128)(2,1)S(1)} %get-tuple-element.113), channel_id=1, source_target_pairs={{0,1},{1,2},{2,3},{3,0},{4,5},{5,6},{6,7},{7,4},{8,9},{9,10},{10,1... | collective-permute-start | bytes 115208 | tf_op jit(solution)/shard_map/ppermute | solution.py:335
  280.5 24.9 %collective-permute-start.23 = (bf16[25,768]{1,0:T(8,128)(2,1)S(1)}, bf16[25,768]{1,0:T(8,128)(2,1)S(1)}, u32[]{:S(2)}, u32[]{:S(2)}) collective-permute-start(bf16[25,768]{1,0:T(8,128)(2,1)S(1)} %get-tuple-element.112), channel_id=1, source_target_pairs={{0,2},{1,3},{2,0},{3,1},{4,6},{5,7},{6,4},{7,5},{8,10},{9,11},{10,... | collective-permute-start | bytes 115208 | tf_op jit(solution)/shard_map/ppermute | solution.py:335
  284.5 20.9 %collective-permute-start.24 = (bf16[25,768]{1,0:T(8,128)(2,1)S(1)}, bf16[25,768]{1,0:T(8,128)(2,1)S(1)}, u32[]{:S(2)}, u32[]{:S(2)}) collective-permute-start(bf16[25,768]{1,0:T(8,128)(2,1)S(1)} %get-tuple-element.111), channel_id=1, source_target_pairs={{0,3},{1,0},{2,1},{3,2},{4,7},{5,4},{6,5},{7,6},{8,11},{9,8},{10,9... | collective-permute-start | bytes 115208 | tf_op jit(solution)/shard_map/ppermute | solution.py:335
  300.9 17.7 %collective-permute-start.13 = (bf16[512,768]{1,0:T(8,128)(2,1)}, bf16[512,768]{1,0:T(8,128)(2,1)}, u32[]{:S(2)}, u32[]{:S(2)}) collective-permute-start(bf16[512,768]{1,0:T(8,128)(2,1)} %get-tuple-element.92), channel_id=1, source_target_pairs={{0,1},{1,2},{4,5},{5,6},{8,9},{9,10},{12,13},{13,14},{16,17},{17,1... | collective-permute-start | bytes 2359304 | tf_op jit(solution)/shard_map/ppermute | solution.py:338
  303.8 14.7 %collective-permute-start.15 = (bf16[512,768]{1,0:T(8,128)(2,1)}, bf16[512,768]{1,0:T(8,128)(2,1)}, u32[]{:S(2)}, u32[]{:S(2)}) collective-permute-start(bf16[512,768]{1,0:T(8,128)(2,1)} %get-tuple-element.91), channel_id=1, source_target_pairs={{2,1},{3,2},{6,5},{7,6},{10,9},{11,10},{14,13},{15,14},{18,17},{19... | collective-permute-start | bytes 2359304 | tf_op jit(solution)/shard_map/ppermute | solution.py:338
  308.2 22.9 %copy-start.5 = (bf16[8,4,24,768]{3,2,1,0:T(8,128)(2,1)S(1)}, bf16[8,4,24,768]{3,2,1,0:T(8,128)(2,1)}, u32[]{:S(2)}) copy-start(bf16[8,4,24,768]{3,2,1,0:T(8,128)(2,1)} %copy-done.4) | copy-start | bytes 3538948
  322.0 34.5 %collective-permute-start.17 = (bf16[512,768]{1,0:T(8,128)(2,1)}, bf16[512,768]{1,0:T(8,128)(2,1)}, u32[]{:S(2)}, u32[]{:S(2)}) collective-permute-start(bf16[512,768]{1,0:T(8,128)(2,1)} %get-tuple-element.90), channel_id=1, source_target_pairs={{1,0},{2,1},{3,2},{5,4},{6,5},{7,6},{9,8},{10,9},{11,10},{13,12},{... | collective-permute-start | bytes 2359304 | tf_op jit(solution)/shard_map/ppermute | solution.py:338
  323.3 33.2 %collective-permute-start.16 = (bf16[512,768]{1,0:T(8,128)(2,1)}, bf16[512,768]{1,0:T(8,128)(2,1)}, u32[]{:S(2)}, u32[]{:S(2)}) collective-permute-start(bf16[512,768]{1,0:T(8,128)(2,1)} %get-tuple-element.89), channel_id=1, source_target_pairs={{0,1},{1,2},{2,3},{4,5},{5,6},{6,7},{8,9},{9,10},{10,11},{12,13},{... | collective-permute-start | bytes 2359304 | tf_op jit(solution)/shard_map/ppermute | solution.py:338
  332.4 2.6 copy-start.10
  332.4 2.6 copy-start.11
  335.0 6.0 %copy-start.22 = (f32[768]{0:T(1024)S(1)}, f32[768]{0:T(1024)}, u32[]{:S(2)}) copy-start(f32[768]{0:T(1024)} %add.368) | copy-start | bytes 9220
  337.3 3.7 %copy-start.12 = (bf16[512,768]{1,0:T(8,128)(2,1)S(1)}, bf16[512,768]{1,0:T(8,128)(2,1)}, u32[]{:S(2)}) copy-start(bf16[512,768]{1,0:T(8,128)(2,1)} %reduce-scatter.3.cloned.1.call-done) | copy-start | bytes 2359300
  338.4 13.7 %collective-permute-start.18 = (bf16[25,768]{1,0:T(8,128)(2,1)S(1)}, bf16[25,768]{1,0:T(8,128)(2,1)S(1)}, u32[]{:S(2)}, u32[]{:S(2)}) collective-permute-start(bf16[25,768]{1,0:T(8,128)(2,1)S(1)} %get-tuple-element.117), channel_id=1, source_target_pairs={{0,1},{1,2},{2,3},{3,0},{4,5},{5,6},{6,7},{7,4},{8,9},{9,10},{10,1... | collective-permute-start | bytes 115208 | tf_op jit(solution)/shard_map/ppermute | solution.py:335
  340.4 9.3 %collective-permute-start.21 = (bf16[24,768]{1,0:T(8,128)(2,1)S(1)}, bf16[24,768]{1,0:T(8,128)(2,1)S(1)}, u32[]{:S(2)}, u32[]{:S(2)}) collective-permute-start(bf16[24,768]{1,0:T(8,128)(2,1)S(1)} %slice.235), channel_id=1, source_target_pairs={{0,0},{1,8},{2,16},{3,24},{4,1},{5,9},{6,17},{7,25},{8,2},{9,10},{... | collective-permute-start | bytes 110600 | tf_op jit(solution)/shard_map/ppermute | solution.py:503
  344.4 7.9 %collective-permute-start.19 = (bf16[25,768]{1,0:T(8,128)(2,1)S(1)}, bf16[25,768]{1,0:T(8,128)(2,1)S(1)}, u32[]{:S(2)}, u32[]{:S(2)}) collective-permute-start(bf16[25,768]{1,0:T(8,128)(2,1)S(1)} %get-tuple-element.116), channel_id=1, source_target_pairs={{0,2},{1,3},{2,0},{3,1},{4,6},{5,7},{6,4},{7,5},{8,10},{9,11},{10,... | collective-permute-start | bytes 115208 | tf_op jit(solution)/shard_map/ppermute | solution.py:335
  349.6 4.4 %collective-permute-start.20 = (bf16[25,768]{1,0:T(8,128)(2,1)S(1)}, bf16[25,768]{1,0:T(8,128)(2,1)S(1)}, u32[]{:S(2)}, u32[]{:S(2)}) collective-permute-start(bf16[25,768]{1,0:T(8,128)(2,1)S(1)} %get-tuple-element.115), channel_id=1, source_target_pairs={{0,3},{1,0},{2,1},{3,2},{4,7},{5,4},{6,5},{7,6},{8,11},{9,8},{10,9... | collective-permute-start | bytes 115208 | tf_op jit(solution)/shard_map/ppermute | solution.py:335
  352.1 4.4 %copy-start.19 = (f32[512]{0:T(512)S(1)}, f32[512]{0:T(512)}, u32[]{:S(2)}) copy-start(f32[512]{0:T(512)} %copy-done.18) | copy-start | bytes 6148
  352.1 4.4 %copy-start.21 = (f32[512]{0:T(512)S(1)}, f32[512]{0:T(512)}, u32[]{:S(2)}) copy-start(f32[512]{0:T(512)} %add_rsqrt_fusion) | copy-start | bytes 6148
  356.5 2.4 copy-start.3
Sparse Core Ops, SparseCore 0:
  68.2 27.7 all-gather.2
  98.4 33.1 all-gather.4
  185.6 58.5 reduce-scatter.2
  280.6 40.0 reduce-scatter.4
where the time goes:
time: 370 us; the launch traced here: 369 us
  waiting for transfers between devices  131 us (35%)
  Pallas kernels  88.2 us (24%)
  starting transfers between devices  58.1 us (16%)
  other arithmetic  37.9 us (10%)
  local copies, waits for them, and re-layouts  30.2 us (8%)
  between operations  15 us (4%)
  matrix products  8.78 us (2%)
    ppermute x12, waiting for transfers between devices, hop(): return lax.ppermute(x, 'seq', pairs)  99.3 us
    pallas_call x1, Pallas kernels, attend(): pl.pallas_call(kernel, out_shape=(jax.ShapeDtypeStruct((n, c, width), BF)...  44.1 us
    ppermute x12, starting transfers between devices, hop(): return lax.ppermute(x, 'seq', pairs)  31.5 us
    pallas_call x1, Pallas kernels, feed(): pl.pallas_call(kernel, grid_spec=pltpu.PrefetchScalarGridSpec(num_scalar_...  29.8 us
    ppermute x12, waiting for transfers between devices, send(): return lax.ppermute(x, 'seq', [(i, (i + k) % n) for i in range(n)])  26.3 us
    ppermute x12, starting transfers between devices, send(): return lax.ppermute(x, 'seq', [(i, (i + k) % n) for i in range(n)])  22.1 us
    pallas_call x1, Pallas kernels, finish(): pl.pallas_call(kernel, grid=(n, c // BLK), in_specs=[tokens_spec(a.shape[...  14.3 us
    dot_general x4, matrix products, nn(): lax.dot_general(a, b, (((1,), (0,)), ((), ())), preferred_element_type=F32)  8.78 us
  transfers between devices with their start and end apart: 30, of which 12 were waited for; matrix products, arithmetic and copies ran while one was open for 17% of the time, Pallas kernels for 16%

commit v1 on v0

--- a/solution.py
+++ b/solution.py
@@ -12,6 +12,7 @@
 mask_fill = -1e30
 eps = 1e-05
 BLK = 256
+TOK = 512
 F32 = jnp.float32
 BF = jnp.bfloat16
 
@@ -176,7 +177,7 @@
 
 
 def tokens_spec(size):
-    return pl.BlockSpec((None, BLK, size), lambda i, j, *_: (i, j, 0))
+    return pl.BlockSpec((None, TOK, size), lambda i, j, *_: (i, j, 0))
 
 
 def whole_spec(shape):
@@ -184,7 +185,7 @@
 
 
 def rows8(v):
-    return jnp.sum(v.reshape(BLK // 8, 8, v.shape[1]), axis=0)
+    return jnp.sum(v.reshape(TOK // 8, 8, v.shape[1]), axis=0)
 
 
 def spread_out(ref, totals, nf):
@@ -204,7 +205,7 @@
 def feed(nf, spare, rank, toks, cots, norms, weights, b_qkv, w_out, b_up):
     n, c, d = toks.shape
     wide, width, hid = b_qkv.shape[1], w_out.shape[0], b_up.shape[1]
-    last = n * (c // BLK) - 1
+    last = n * (c // TOK) - 1
     tall = (d + hid) // nf + spare
 
     def kernel(
@@ -214,7 +215,7 @@
         w_up = w_ref[:, :hid]
         w_down = w_ref[:, hid : hid + d]
         w_qkv = w_ref[:, hid + d :]
-        step = pl.program_id(0) * (c // BLK) + pl.program_id(1)
+        step = pl.program_id(0) * (c // TOK) + pl.program_id(1)
 
         @pl.when(step == 0)
         def _():
@@ -250,11 +251,11 @@
         kernel,
         grid_spec=pltpu.PrefetchScalarGridSpec(
             num_scalar_prefetch=1,
-            grid=(n, c // BLK),
+            grid=(n, c // TOK),
             in_specs=[tokens_spec(d)] * 2 + [whole_spec(a.shape) for a in ins[2:]],
             out_specs=(
                 tokens_spec(wide), tokens_spec(width),
-                pl.BlockSpec((None, BLK, d), lambda i, j, r: (lax.rem(r[0] - i + n, n), j, 0)),
+                pl.BlockSpec((None, TOK, d), lambda i, j, r: (lax.rem(r[0] - i + n, n), j, 0)),
                 tokens_spec(d),
                 whole_spec((nf, tall, d)), whole_spec((2, 8, d)), whole_spec((8, hid)),
             ),
@@ -281,13 +282,13 @@
 def finish(nf, tall, toks, cots, rest, grad_proj, mixed, norms, weights):
     n, c, d = toks.shape
     wide, width = grad_proj.shape[2], mixed.shape[2]
-    last = n * (c // BLK) - 1
+    last = n * (c // TOK) - 1
 
     def kernel(
         x_ref, cot_ref, rest_ref, gp_ref, mixed_ref, norm_ref, wq_ref,
         q_ref, all_ref, sum_ref, aq, ao,
     ):
-        step = pl.program_id(0) * (c // BLK) + pl.program_id(1)
+        step = pl.program_id(0) * (c // TOK) + pl.program_id(1)
 
         @pl.when(step == 0)
         def _():
@@ -311,7 +312,7 @@
     ins = (toks, cots, rest, grad_proj, mixed, norms, weights)
     return pl.pallas_call(
         kernel,
-        grid=(n, c // BLK),
+        grid=(n, c // TOK),
         in_specs=[tokens_spec(a.shape[2]) for a in ins[:5]] + [whole_spec(a.shape) for a in ins[5:]],
         out_specs=(tokens_spec(d), whole_spec((nf, tall, d)), whole_spec((2, 8, d))),
         out_shape=(

time: 370 us -> 374 us (1.011); the launches traced: 369 us -> 368 us
  no operation moved by 1% of the time
where the time goes in v1:
time: 374 us; the launch traced here: 368 us
  waiting for transfers between devices  132 us (35%)
  Pallas kernels  85.2 us (23%)
  starting transfers between devices  58.4 us (16%)
  other arithmetic  37.9 us (10%)
  local copies, waits for them, and re-layouts  30.2 us (8%)
  between operations  15.4 us (4%)
  matrix products  8.79 us (2%)
    ppermute x12, waiting for transfers between devices, hop(): return lax.ppermute(x, 'seq', pairs)  99.3 us
    pallas_call x1, Pallas kernels, attend(): pl.pallas_call(kernel, out_shape=(jax.ShapeDtypeStruct((n, c, width), BF)...  44.3 us
    ppermute x12, starting transfers between devices, hop(): return lax.ppermute(x, 'seq', pairs)  31.4 us
    pallas_call x1, Pallas kernels, feed(): pl.pallas_call(kernel, grid_spec=pltpu.PrefetchScalarGridSpec(num_scalar_...  28 us
    ppermute x12, waiting for transfers between devices, send(): return lax.ppermute(x, 'seq', [(i, (i + k) % n) for i in range(n)])  27.7 us
    ppermute x12, starting transfers between devices, send(): return lax.ppermute(x, 'seq', [(i, (i + k) % n) for i in range(n)])  22.4 us
    pallas_call x1, Pallas kernels, finish(): pl.pallas_call(kernel, grid=(n, c // TOK), in_specs=[tokens_spec(a.shape[...  12.9 us
    dot_general x4, matrix products, nn(): lax.dot_general(a, b, (((1,), (0,)), ((), ())), preferred_element_type=F32)  8.79 us
  transfers between devices with their start and end apart: 30, of which 12 were waited for; matrix products, arithmetic and copies ran while one was open for 17% of the time, Pallas kernels for 16%

profile of v1, /device:TPU:0, one launch (start us, length us, event | category | flops | bytes accessed | tf_op | source)
XLA Modules:
  0.0 367.6 jit_solution(5787350976685444337)
XLA Ops:
  7.2 2.1 constant_dynamic-update-slice_fusion.1
  9.5 1.6 fusion.76
  11.1 5.0 %collective-permute-start = (bf16[2,512,768]{2,1,0:T(8,128)(2,1)}, bf16[2,512,768]{2,1,0:T(8,128)(2,1)S(1)}, u32[]{:S(2)}, u32[]{:S(2)}) collective-permute-start(bf16[2,512,768]{2,1,0:T(8,128)(2,1)} %get-tuple-element.106), channel_id=1, source_target_pairs={{0,1},{1,2},{2,3},{4,5},{5,6},{6,7},{8,9},{9,10},{10,11},{12,13},{... | collective-permute-start | bytes 4718600 | tf_op jit(solution)/shard_map/ppermute | solution.py:339
  16.1 1.3 collective-permute-start.1
  18.8 3.8 %fusion.35 = (f32[1,512,128]{2,1,0:T(8,128)S(1)}, f32[1,512,128]{2,1,0:T(8,128)S(1)}, f32[1,512,128]{2,1,0:T(8,128)S(1)}, f32[1,512,128]{2,1,0:T(8,128)S(1)}, f3...) fusion(f32[512]{0:T(512)S(1)} %get-tuple-element.148, ...), kind=kLoop, calls=%fused_computation.66 | loop fusion | flops 1310720 | bytes 3154816 | tf_op jit(solution)/shard_map/jit(_where)/select_n | solution.py:28
  22.7 1.0 pad_maximum_fusion.2.c_ref
  23.7 1.1 pad_maximum_fusion.3.sa_ref
  24.8 1.1 pad_maximum_fusion.4.sb_ref
  25.9 24.0 %collective-permute-done = bf16[2,512,768]{2,1,0:T(8,128)(2,1)S(1)} collective-permute-done((bf16[2,512,768]{2,1,0:T(8,128)(2,1)}, bf16[2,512,768]{2,1,0:T(8,128)(2,1)S(1)}, u32[]{:S(2)}, u32[]{:S(2)}) %collective-permute-start) | collective-permute-done | bytes 1572896 | tf_op jit(solution)/shard_map/ppermute | solution.py:339
  50.0 4.2 %collective-permute-done.1 = bf16[2,512,768]{2,1,0:T(8,128)(2,1)} collective-permute-done((bf16[2,512,768]{2,1,0:T(8,128)(2,1)}, bf16[2,512,768]{2,1,0:T(8,128)(2,1)}, u32[]{:S(2)}, u32[]{:S(2)}) %collective-permute-start.1) | collective-permute-done | bytes 1572896 | tf_op jit(solution)/shard_map/ppermute | solution.py:339
  54.9 1.5 collective-permute-start.2
  56.4 1.0 collective-permute-start.3
  57.4 2.9 collective-permute-start.4
  60.4 3.4 collective-permute-done.2
  64.6 2.6 collective-permute-done.3
  69.1 1.8 collective-permute-start.7
  70.9 1.3 collective-permute-start.5
  72.2 1.9 collective-permute-start.8
  74.1 37.6 %collective-permute-done.5 = bf16[2,512,768]{2,1,0:T(8,128)(2,1)} collective-permute-done((bf16[2,512,768]{2,1,0:T(8,128)(2,1)}, bf16[2,512,768]{2,1,0:T(8,128)(2,1)}, u32[]{:S(2)}, u32[]{:S(2)}) %collective-permute-start.5) | collective-permute-done | bytes 1572896 | tf_op jit(solution)/shard_map/ppermute | solution.py:339
  111.7 1.5 collective-permute-start.6
  113.2 1.6 broadcast_select_fusion.1
  115.7 1.4 slice.225
  118.0 1.7 fusion.62
  123.9 1.6 broadcast_select_fusion
  125.7 23.1 %collective-permute-done.6 = bf16[2,512,768]{2,1,0:T(8,128)(2,1)} collective-permute-done((bf16[2,512,768]{2,1,0:T(8,128)(2,1)}, bf16[2,512,768]{2,1,0:T(8,128)(2,1)}, u32[]{:S(2)}, u32[]{:S(2)}) %collective-permute-start.6) | collective-permute-done | bytes 1572896 | tf_op jit(solution)/shard_map/ppermute | solution.py:339
  148.7 1.6 broadcast_select_fusion.2
  150.5 1.0 copy-done
  151.7 1.9 pad_maximum_fusion.x_ref
  153.6 1.9 pad_maximum_fusion.1.cot_ref
  155.6 28.0 %feed.1 = (f32[4,512,576]{2,1,0:T(8,128)}, bf16[4,512,192]{2,1,0:T(8,128)(2,1)}, bf16[4,512,768]{2,1,0:T(8,128)(2,1)}, bf16[4,512,768]{2,1,0:T(8,128)(2,1)}, bf1...) custom-call(s32[1]{0:T(128)} %bitcast.11.rank_ref, bf16[4,512,768]{2,1,0:T(8,128)(2,1)} %pad_maximum_fusion.x_ref, ...), custom_call_target="tpu_custom_call" | custom-call | flops 16911433728 | bytes 31457280 | tf_op jit(solution)/shard_map/feed/pallas_call | solution.py:250
  185.0 1.6 dynamic_update_slice.48
  186.6 3.7 %all-to-all-start = ((bf16[8,208,768]{2,1,0:T(8,128)(2,1)}), bf16[8,208,768]{2,1,0:T(8,128)(2,1)S(1)}, u32[]{:S(2)}, u32[]{:S(2)}) async-start(bf16[8,208,768]{2,1,0:T(8,128)(2,1)} %dynamic_update_slice.48), calls=%async_computation.1 | async-start | bytes 5111808 | tf_op jit(solution)/shard_map/all_to_all | solution.py:481
  192.2 44.3 %attend.1 = (bf16[4,512,192]{2,1,0:T(8,128)(2,1)}, bf16[4,512,576]{2,1,0:T(8,128)(2,1)}, f32[8,576]{1,0:T(8,128)}) custom-call(s32[1]{0:T(128)} %bitcast.11.rank_ref, f32[4,512,576]{2,1,0:T(8,128)} %get-tuple-element.53.proj_ref, bf16[4,512,192]{2,1,0:T(8,128)(2,1)} %get-tuple-element.54.gm_ref, f32[4,512,128]{2,1,0:T(8,128)} %pad_maximum_fusion.2.c_ref, ...), custom_call_target="tpu_custom_call" | custom-call | flops 4831838208 | bytes 16777216 | tf_op jit(solution)/shard_map/attend/pallas_call | solution.py:147
  237.6 4.6 %reduce-scatter.3.cloned.1.call-done = bf16[512,768]{1,0:T(8,128)(2,1)} async-done(((bf16[2048,768]{1,0:T(8,128)(2,1)}), bf16[512,768]{1,0:T(8,128)(2,1)}) %reduce-scatter.3.cloned.1.call-update) | async-done | bytes 786448 | tf_op jit(solution)/shard_map/reduce_scatter | solution.py:472
  242.2 2.2 slice_bitcast_fusion.2
  244.4 2.3 collective-permute-start.9
  247.2 1.9 collective-permute-start.11
  249.1 12.9 %finish.1 = (bf16[4,512,768]{2,1,0:T(8,128)(2,1)}, bf16[8,128,768]{2,1,0:T(8,128)(2,1)}, f32[2,8,768]{2,1,0:T(8,128)}) custom-call(bf16[4,512,768]{2,1,0:T(8,128)(2,1)} %pad_maximum_fusion.x_ref, bf16[4,512,768]{2,1,0:T(8,128)(2,1)} %pad_maximum_fusion.1.cot_ref, bf16[4,512,768]{2,1,0:T(8,128)(2,1)} %get-tuple-element.62.rest_ref, ...), custom_call_target="tpu_custom_call" | custom-call | flops 1572864 | bytes 1572864 | tf_op jit(solution)/shard_map/finish/pallas_call | solution.py:313
  262.9 1.2 convert_reduce_fusion
  264.0 6.6 %collective-permute-done.10 = bf16[512,192]{1,0:T(8,128)(2,1)} collective-permute-done((bf16[512,192]{1,0:T(8,128)(2,1)}, bf16[512,192]{1,0:T(8,128)(2,1)}, u32[]{:S(2)}, u32[]{:S(2)}) %collective-permute-start.10) | collective-permute-done | bytes 196640 | tf_op jit(solution)/shard_map/ppermute | solution.py:336
  270.8 1.7 collective-permute-start.14
  272.5 3.3 collective-permute-start.12
  277.3 1.6 dynamic_update_slice.49
  278.9 4.0 %collective-permute-start.23 = (bf16[25,768]{1,0:T(8,128)(2,1)S(1)}, bf16[25,768]{1,0:T(8,128)(2,1)S(1)}, u32[]{:S(2)}, u32[]{:S(2)}) collective-permute-start(bf16[25,768]{1,0:T(8,128)(2,1)S(1)} %get-tuple-element.112), channel_id=1, source_target_pairs={{0,2},{1,3},{2,0},{3,1},{4,6},{5,7},{6,4},{7,5},{8,10},{9,11},{10,... | collective-permute-start | bytes 115208 | tf_op jit(solution)/shard_map/ppermute | solution.py:336
  282.9 13.2 %collective-permute-done.22 = bf16[25,768]{1,0:T(8,128)(2,1)S(1)} collective-permute-done((bf16[25,768]{1,0:T(8,128)(2,1)S(1)}, bf16[25,768]{1,0:T(8,128)(2,1)S(1)}, u32[]{:S(2)}, u32[]{:S(2)}) %collective-permute-start.22) | collective-permute-done | bytes 38432 | tf_op jit(solution)/shard_map/ppermute | solution.py:336
  296.2 3.1 fusion.19
  299.3 3.0 collective-permute-start.13
  302.2 1.5 collective-permute-start.15
  304.3 1.1 reshape.1138
  306.6 10.4 %collective-permute-done.13 = bf16[512,768]{1,0:T(8,128)(2,1)} collective-permute-done((bf16[512,768]{1,0:T(8,128)(2,1)}, bf16[512,768]{1,0:T(8,128)(2,1)}, u32[]{:S(2)}, u32[]{:S(2)}) %collective-permute-start.13) | collective-permute-done | bytes 786464 | tf_op jit(solution)/shard_map/ppermute | solution.py:339
  317.0 3.4 add_convert_fusion.1
  320.4 1.3 collective-permute-start.17
  321.7 7.8 %collective-permute-start.16 = (bf16[512,768]{1,0:T(8,128)(2,1)}, bf16[512,768]{1,0:T(8,128)(2,1)}, u32[]{:S(2)}, u32[]{:S(2)}) collective-permute-start(bf16[512,768]{1,0:T(8,128)(2,1)} %get-tuple-element.89), channel_id=1, source_target_pairs={{0,1},{1,2},{2,3},{4,5},{5,6},{6,7},{8,9},{9,10},{10,11},{12,13},{... | collective-permute-start | bytes 2359304 | tf_op jit(solution)/shard_map/ppermute | solution.py:339
  329.5 1.3 fusion.41
  330.8 2.5 fusion.43
  333.4 1.5 fusion.79
  335.7 1.0 slice.231
  336.8 1.2 collective-permute-start.18
  339.4 3.4 fusion.23
  342.8 5.1 %collective-permute-start.19 = (bf16[25,768]{1,0:T(8,128)(2,1)S(1)}, bf16[25,768]{1,0:T(8,128)(2,1)S(1)}, u32[]{:S(2)}, u32[]{:S(2)}) collective-permute-start(bf16[25,768]{1,0:T(8,128)(2,1)S(1)} %get-tuple-element.116), channel_id=1, source_target_pairs={{0,2},{1,3},{2,0},{3,1},{4,6},{5,7},{6,4},{7,5},{8,10},{9,11},{10,... | collective-permute-start | bytes 115208 | tf_op jit(solution)/shard_map/ppermute | solution.py:336
  348.0 1.9 collective-permute-start.20
  350.7 1.8 collective-permute-done.20
  354.9 2.4 fusion.53
  357.3 3.3 fusion.24
  (217 shorter events, 25.4 us)
Async XLA Ops:
  7.2 2.2 copy-start.2
  7.2 10.3 %copy-start.15 = (bf16[24,2304]{1,0:T(8,128)(2,1)S(1)}, bf16[24,2304]{1,0:T(8,128)(2,1)}, u32[]{:S(2)}) copy-start(bf16[24,2304]{1,0:T(8,128)(2,1)} %param.16) | copy-start | bytes 331780
  7.2 108.5 %all-gather.3.cloned.1.call-start = ((), (), s32[]{:S(2)}) async-start(), calls=%async_computation.3 | async-start | bytes 1769472 | tf_op jit(solution)/shard_map/all_gather | solution.py:442
  9.4 8.6 %copy-start.14 = (bf16[24,3072]{1,0:T(8,128)(2,1)S(1)}, bf16[24,3072]{1,0:T(8,128)(2,1)}, u32[]{:S(2)}) copy-start(bf16[24,3072]{1,0:T(8,128)(2,1)} %param.20) | copy-start | bytes 442372
  9.4 9.0 %copy-start.24 = (bf16[72]{0:T(256)(128)(2,1)S(1)}, bf16[72]{0:T(256)(128)(2,1)}, u32[]{:S(2)}) copy-start(bf16[72]{0:T(256)(128)(2,1)} %param.17) | copy-start | bytes 436
  9.4 9.0 %copy-start.25 = (bf16[24]{0:T(256)(128)(2,1)S(1)}, bf16[24]{0:T(256)(128)(2,1)}, u32[]{:S(2)}) copy-start(bf16[24]{0:T(256)(128)(2,1)} %param.19) | copy-start | bytes 148
  9.4 9.0 %copy-start.26 = (bf16[96]{0:T(256)(128)(2,1)S(1)}, bf16[96]{0:T(256)(128)(2,1)}, u32[]{:S(2)}) copy-start(bf16[96]{0:T(256)(128)(2,1)} %param.21) | copy-start | bytes 580
  9.4 9.1 %copy-start.27 = (bf16[24]{0:T(256)(128)(2,1)S(1)}, bf16[24]{0:T(256)(128)(2,1)}, u32[]{:S(2)}) copy-start(bf16[24]{0:T(256)(128)(2,1)} %param.23) | copy-start | bytes 148
  9.4 9.1 %copy-start.28 = (bf16[24]{0:T(256)(128)(2,1)S(1)}, bf16[24]{0:T(256)(128)(2,1)}, u32[]{:S(2)}) copy-start(bf16[24]{0:T(256)(128)(2,1)} %param.24) | copy-start | bytes 148
  9.4 9.1 %copy-start.29 = (bf16[24]{0:T(256)(128)(2,1)S(1)}, bf16[24]{0:T(256)(128)(2,1)}, u32[]{:S(2)}) copy-start(bf16[24]{0:T(256)(128)(2,1)} %param.25) | copy-start | bytes 148
  9.5 9.1 %copy-start.30 = (bf16[24]{0:T(256)(128)(2,1)S(1)}, bf16[24]{0:T(256)(128)(2,1)}, u32[]{:S(2)}) copy-start(bf16[24]{0:T(256)(128)(2,1)} %param.26) | copy-start | bytes 148
  9.5 9.1 %copy-start.31 = (bf16[24]{0:T(256)(128)(2,1)S(1)}, bf16[24]{0:T(256)(128)(2,1)}, u32[]{:S(2)}) copy-start(bf16[24]{0:T(256)(128)(2,1)} %param.27) | copy-start | bytes 148
  9.5 9.2 %copy-start.17 = (bf16[24,768]{1,0:T(8,128)(2,1)S(1)}, bf16[24,768]{1,0:T(8,128)(2,1)}, u32[]{:S(2)}) copy-start(bf16[24,768]{1,0:T(8,128)(2,1)} %param.18) | copy-start | bytes 110596
  11.1 38.9 %collective-permute-start = (bf16[2,512,768]{2,1,0:T(8,128)(2,1)}, bf16[2,512,768]{2,1,0:T(8,128)(2,1)S(1)}, u32[]{:S(2)}, u32[]{:S(2)}) collective-permute-start(bf16[2,512,768]{2,1,0:T(8,128)(2,1)} %get-tuple-element.106), channel_id=1, source_target_pairs={{0,1},{1,2},{2,3},{4,5},{5,6},{6,7},{8,9},{9,10},{10,11},{12,13},{... | collective-permute-start | bytes 4718600 | tf_op jit(solution)/shard_map/ppermute | solution.py:339
  16.1 38.1 %collective-permute-start.1 = (bf16[2,512,768]{2,1,0:T(8,128)(2,1)}, bf16[2,512,768]{2,1,0:T(8,128)(2,1)}, u32[]{:S(2)}, u32[]{:S(2)}) collective-permute-start(bf16[2,512,768]{2,1,0:T(8,128)(2,1)} %get-tuple-element.106), channel_id=1, source_target_pairs={{1,0},{2,1},{3,2},{5,4},{6,5},{7,6},{9,8},{10,9},{11,10},{13,12},{... | collective-permute-start | bytes 4718600 | tf_op jit(solution)/shard_map/ppermute | solution.py:339
  50.0 19.1 %copy-start.8 = (bf16[2,512,768]{2,1,0:T(8,128)(2,1)}, bf16[2,512,768]{2,1,0:T(8,128)(2,1)S(1)}, u32[]{:S(2)}) copy-start(bf16[2,512,768]{2,1,0:T(8,128)(2,1)S(1)} %collective-permute-done) | copy-start | bytes 4718596
  54.2 14.0 %copy-start.13 = (bf16[96,768]{1,0:T(8,128)(2,1)S(1)}, bf16[96,768]{1,0:T(8,128)(2,1)}, u32[]{:S(2)}) copy-start(bf16[96,768]{1,0:T(8,128)(2,1)} %param.22) | copy-start | bytes 442372
  54.9 8.8 %collective-permute-start.2 = (bf16[32,2112]{1,0:T(8,128)(2,1)}, bf16[32,2112]{1,0:T(8,128)(2,1)}, u32[]{:S(2)}, u32[]{:S(2)}) collective-permute-start(bf16[32,2112]{1,0:T(8,128)(2,1)} %get-tuple-element.109), channel_id=1, source_target_pairs={{0,1},{1,2},{2,3},{3,0},{4,5},{5,6},{6,7},{7,4},{8,9},{9,10},{10,1... | collective-permute-start | bytes 405512 | tf_op jit(solution)/shard_map/ppermute | solution.py:336
  56.4 10.9 %collective-permute-start.3 = (bf16[32,2112]{1,0:T(8,128)(2,1)S(1)}, bf16[32,2112]{1,0:T(8,128)(2,1)S(1)}, u32[]{:S(2)}, u32[]{:S(2)}) collective-permute-start(bf16[32,2112]{1,0:T(8,128)(2,1)S(1)} %get-tuple-element.108), channel_id=1, source_target_pairs={{0,2},{1,3},{2,0},{3,1},{4,6},{5,7},{6,4},{7,5},{8,10},{9,11},{10,... | collective-permute-start | bytes 405512 | tf_op jit(solution)/shard_map/ppermute | solution.py:336
  57.4 9.9 %collective-permute-start.4 = (bf16[32,2112]{1,0:T(8,128)(2,1)S(1)}, bf16[32,2112]{1,0:T(8,128)(2,1)S(1)}, u32[]{:S(2)}, u32[]{:S(2)}) collective-permute-start(bf16[32,2112]{1,0:T(8,128)(2,1)S(1)} %get-tuple-element.107), channel_id=1, source_target_pairs={{0,3},{1,0},{2,1},{3,2},{4,7},{5,4},{6,5},{7,6},{8,11},{9,8},{10,9... | collective-permute-start | bytes 405512 | tf_op jit(solution)/shard_map/ppermute | solution.py:336
  68.1 87.5 %all-gather.5.cloned.1.call-start = ((), (), s32[]{:S(2)}) async-start(), calls=%async_computation.4 | async-start | bytes 3760128 | tf_op jit(solution)/shard_map/all_gather | solution.py:446
  69.0 173.2 %reduce-scatter.3.cloned.1.call-start = ((), (), s32[]{:S(2)}) async-start(), calls=%async_computation.5 | async-start | bytes 3932160 | tf_op jit(solution)/shard_map/reduce_scatter | solution.py:472
  69.1 3.1 collective-permute-start.7
  70.9 40.8 %collective-permute-start.5 = (bf16[2,512,768]{2,1,0:T(8,128)(2,1)}, bf16[2,512,768]{2,1,0:T(8,128)(2,1)}, u32[]{:S(2)}, u32[]{:S(2)}) collective-permute-start(bf16[2,512,768]{2,1,0:T(8,128)(2,1)} %collective-permute-done.1), channel_id=1, source_target_pairs={{1,0},{2,1},{5,4},{6,5},{9,8},{10,9},{13,12},{14,13},{17,16},{18,1... | collective-permute-start | bytes 4718600 | tf_op jit(solution)/shard_map/ppermute | solution.py:339
  72.2 51.8 %collective-permute-start.8 = (bf16[2,512,768]{2,1,0:T(8,128)(2,1)}, bf16[2,512,768]{2,1,0:T(8,128)(2,1)}, u32[]{:S(2)}, u32[]{:S(2)}) collective-permute-start(bf16[2,512,768]{2,1,0:T(8,128)(2,1)} %collective-permute-done.7), channel_id=1, source_target_pairs={{2,3},{6,7},{10,11},{14,15},{18,19},{22,23},{26,27},{30,31}} | collective-permute-start | bytes 4718600 | tf_op jit(solution)/shard_map/ppermute | solution.py:339
  111.7 37.0 %collective-permute-start.6 = (bf16[2,512,768]{2,1,0:T(8,128)(2,1)}, bf16[2,512,768]{2,1,0:T(8,128)(2,1)}, u32[]{:S(2)}, u32[]{:S(2)}) collective-permute-start(bf16[2,512,768]{2,1,0:T(8,128)(2,1)} %collective-permute-done.5), channel_id=1, source_target_pairs={{1,0},{5,4},{9,8},{13,12},{17,16},{21,20},{25,24},{29,28}} | collective-permute-start | bytes 4718600 | tf_op jit(solution)/shard_map/ppermute | solution.py:339
  117.1 8.4 %copy-start.4 = (bf16[8,4,24,768]{3,2,1,0:T(8,128)(2,1)}, bf16[8,4,24,768]{3,2,1,0:T(8,128)(2,1)S(1)}, u32[]{:S(2)}) copy-start(bf16[8,4,24,768]{3,2,1,0:T(8,128)(2,1)S(1)} %slice.225) | copy-start | bytes 3538948
  125.5 23.2 %copy-start.9 = (bf16[2,512,768]{2,1,0:T(8,128)(2,1)S(1)}, bf16[2,512,768]{2,1,0:T(8,128)(2,1)}, u32[]{:S(2)}) copy-start(bf16[2,512,768]{2,1,0:T(8,128)(2,1)} %copy-done.8) | copy-start | bytes 4718596
  150.3 1.1 copy-start
  150.3 1.4 copy-start.7
  183.5 0.7 copy-start.23
  183.5 0.8 copy-start.20
  183.6 0.9 copy-start.16
  186.6 50.9 %all-to-all-start = ((bf16[8,208,768]{2,1,0:T(8,128)(2,1)}), bf16[8,208,768]{2,1,0:T(8,128)(2,1)S(1)}, u32[]{:S(2)}, u32[]{:S(2)}) async-start(bf16[8,208,768]{2,1,0:T(8,128)(2,1)} %dynamic_update_slice.48), calls=%async_computation.1 | async-start | bytes 5111808 | tf_op jit(solution)/shard_map/all_to_all | solution.py:481
  190.4 144.5 %reduce-scatter.5.cloned.1.call-start = ((), (), s32[]{:S(2)}) async-start(), calls=%async_computation.6 | async-start | bytes 1769472 | tf_op jit(solution)/shard_map/reduce_scatter | solution.py:500
  190.6 45.9 %copy-start.18 = (f32[512]{0:T(512)}, f32[512]{0:T(512)S(1)}, u32[]{:S(2)}) copy-start(f32[512]{0:T(512)S(1)} %broadcast_multiply_fusion.2) | copy-start | bytes 6148
  244.4 19.6 %collective-permute-start.9 = (bf16[512,192]{1,0:T(8,128)(2,1)}, bf16[512,192]{1,0:T(8,128)(2,1)}, u32[]{:S(2)}, u32[]{:S(2)}) collective-permute-start(bf16[512,192]{1,0:T(8,128)(2,1)} %get-tuple-element.103), channel_id=1, source_target_pairs={{0,3},{1,0},{2,1},{3,2},{4,7},{5,4},{6,5},{7,6},{8,11},{9,8},{10,9... | collective-permute-start | bytes 589832 | tf_op jit(solution)/shard_map/ppermute | solution.py:336
  246.7 23.9 %collective-permute-start.10 = (bf16[512,192]{1,0:T(8,128)(2,1)}, bf16[512,192]{1,0:T(8,128)(2,1)}, u32[]{:S(2)}, u32[]{:S(2)}) collective-permute-start(bf16[512,192]{1,0:T(8,128)(2,1)} %get-tuple-element.102), channel_id=1, source_target_pairs={{0,2},{1,3},{2,0},{3,1},{4,6},{5,7},{6,4},{7,5},{8,10},{9,11},{10,... | collective-permute-start | bytes 589832 | tf_op jit(solution)/shard_map/ppermute | solution.py:336
  247.2 23.5 %collective-permute-start.11 = (bf16[512,192]{1,0:T(8,128)(2,1)}, bf16[512,192]{1,0:T(8,128)(2,1)}, u32[]{:S(2)}, u32[]{:S(2)}) collective-permute-start(bf16[512,192]{1,0:T(8,128)(2,1)} %get-tuple-element.101), channel_id=1, source_target_pairs={{0,1},{1,2},{2,3},{3,0},{4,5},{5,6},{6,7},{7,4},{8,9},{9,10},{10,1... | collective-permute-start | bytes 589832 | tf_op jit(solution)/shard_map/ppermute | solution.py:336
  262.9 7.8 %copy-start.1 = (bf16[4,512,768]{2,1,0:T(8,128)(2,1)S(1)}, bf16[4,512,768]{2,1,0:T(8,128)(2,1)}, u32[]{:S(2)}) copy-start(bf16[4,512,768]{2,1,0:T(8,128)(2,1)} %get-tuple-element.69) | copy-start | bytes 9437188
  270.7 5.3 %copy-start.6 = (f32[208,768]{1,0:T(8,128)S(1)}, f32[208,768]{1,0:T(8,128)}, u32[]{:S(2)}) copy-start(f32[208,768]{1,0:T(8,128)} %convert_reduce_fusion) | copy-start | bytes 1916932
  270.8 25.4 %collective-permute-start.14 = (bf16[512,768]{1,0:T(8,128)(2,1)S(1)}, bf16[512,768]{1,0:T(8,128)(2,1)}, u32[]{:S(2)}, u32[]{:S(2)}) collective-permute-start(bf16[512,768]{1,0:T(8,128)(2,1)S(1)} %get-tuple-element.93), channel_id=1, source_target_pairs={{3,2},{7,6},{11,10},{15,14},{19,18},{23,22},{27,26},{31,30}} | collective-permute-start | bytes 2359304 | tf_op jit(solution)/shard_map/ppermute | solution.py:339
  272.5 23.7 %collective-permute-start.12 = (bf16[512,768]{1,0:T(8,128)(2,1)S(1)}, bf16[512,768]{1,0:T(8,128)(2,1)}, u32[]{:S(2)}, u32[]{:S(2)}) collective-permute-start(bf16[512,768]{1,0:T(8,128)(2,1)S(1)} %get-tuple-element.94), channel_id=1, source_target_pairs={{0,1},{4,5},{8,9},{12,13},{16,17},{20,21},{24,25},{28,29}} | collective-permute-start | bytes 2359304 | tf_op jit(solution)/shard_map/ppermute | solution.py:339
  276.3 19.9 %collective-permute-start.22 = (bf16[25,768]{1,0:T(8,128)(2,1)S(1)}, bf16[25,768]{1,0:T(8,128)(2,1)S(1)}, u32[]{:S(2)}, u32[]{:S(2)}) collective-permute-start(bf16[25,768]{1,0:T(8,128)(2,1)S(1)} %get-tuple-element.113), channel_id=1, source_target_pairs={{0,1},{1,2},{2,3},{3,0},{4,5},{5,6},{6,7},{7,4},{8,9},{9,10},{10,1... | collective-permute-start | bytes 115208 | tf_op jit(solution)/shard_map/ppermute | solution.py:336
  278.9 24.9 %collective-permute-start.23 = (bf16[25,768]{1,0:T(8,128)(2,1)S(1)}, bf16[25,768]{1,0:T(8,128)(2,1)S(1)}, u32[]{:S(2)}, u32[]{:S(2)}) collective-permute-start(bf16[25,768]{1,0:T(8,128)(2,1)S(1)} %get-tuple-element.112), channel_id=1, source_target_pairs={{0,2},{1,3},{2,0},{3,1},{4,6},{5,7},{6,4},{7,5},{8,10},{9,11},{10,... | collective-permute-start | bytes 115208 | tf_op jit(solution)/shard_map/ppermute | solution.py:336
  282.9 20.9 %collective-permute-start.24 = (bf16[25,768]{1,0:T(8,128)(2,1)S(1)}, bf16[25,768]{1,0:T(8,128)(2,1)S(1)}, u32[]{:S(2)}, u32[]{:S(2)}) collective-permute-start(bf16[25,768]{1,0:T(8,128)(2,1)S(1)} %get-tuple-element.111), channel_id=1, source_target_pairs={{0,3},{1,0},{2,1},{3,2},{4,7},{5,4},{6,5},{7,6},{8,11},{9,8},{10,9... | collective-permute-start | bytes 115208 | tf_op jit(solution)/shard_map/ppermute | solution.py:336
  299.3 17.7 %collective-permute-start.13 = (bf16[512,768]{1,0:T(8,128)(2,1)}, bf16[512,768]{1,0:T(8,128)(2,1)}, u32[]{:S(2)}, u32[]{:S(2)}) collective-permute-start(bf16[512,768]{1,0:T(8,128)(2,1)} %get-tuple-element.92), channel_id=1, source_target_pairs={{0,1},{1,2},{4,5},{5,6},{8,9},{9,10},{12,13},{13,14},{16,17},{17,1... | collective-permute-start | bytes 2359304 | tf_op jit(solution)/shard_map/ppermute | solution.py:339
  302.2 14.7 %collective-permute-start.15 = (bf16[512,768]{1,0:T(8,128)(2,1)}, bf16[512,768]{1,0:T(8,128)(2,1)}, u32[]{:S(2)}, u32[]{:S(2)}) collective-permute-start(bf16[512,768]{1,0:T(8,128)(2,1)} %get-tuple-element.91), channel_id=1, source_target_pairs={{2,1},{3,2},{6,5},{7,6},{10,9},{11,10},{14,13},{15,14},{18,17},{19... | collective-permute-start | bytes 2359304 | tf_op jit(solution)/shard_map/ppermute | solution.py:339
  306.6 22.9 %copy-start.5 = (bf16[8,4,24,768]{3,2,1,0:T(8,128)(2,1)S(1)}, bf16[8,4,24,768]{3,2,1,0:T(8,128)(2,1)}, u32[]{:S(2)}) copy-start(bf16[8,4,24,768]{3,2,1,0:T(8,128)(2,1)} %copy-done.4) | copy-start | bytes 3538948
  320.4 34.5 %collective-permute-start.17 = (bf16[512,768]{1,0:T(8,128)(2,1)}, bf16[512,768]{1,0:T(8,128)(2,1)}, u32[]{:S(2)}, u32[]{:S(2)}) collective-permute-start(bf16[512,768]{1,0:T(8,128)(2,1)} %get-tuple-element.90), channel_id=1, source_target_pairs={{1,0},{2,1},{3,2},{5,4},{6,5},{7,6},{9,8},{10,9},{11,10},{13,12},{... | collective-permute-start | bytes 2359304 | tf_op jit(solution)/shard_map/ppermute | solution.py:339
  321.7 33.2 %collective-permute-start.16 = (bf16[512,768]{1,0:T(8,128)(2,1)}, bf16[512,768]{1,0:T(8,128)(2,1)}, u32[]{:S(2)}, u32[]{:S(2)}) collective-permute-start(bf16[512,768]{1,0:T(8,128)(2,1)} %get-tuple-element.89), channel_id=1, source_target_pairs={{0,1},{1,2},{2,3},{4,5},{5,6},{6,7},{8,9},{9,10},{10,11},{12,13},{... | collective-permute-start | bytes 2359304 | tf_op jit(solution)/shard_map/ppermute | solution.py:339
  330.8 2.6 copy-start.10
  330.8 2.6 copy-start.11
  333.4 6.0 %copy-start.22 = (f32[768]{0:T(1024)S(1)}, f32[768]{0:T(1024)}, u32[]{:S(2)}) copy-start(f32[768]{0:T(1024)} %add.368) | copy-start | bytes 9220
  335.7 3.7 %copy-start.12 = (bf16[512,768]{1,0:T(8,128)(2,1)S(1)}, bf16[512,768]{1,0:T(8,128)(2,1)}, u32[]{:S(2)}) copy-start(bf16[512,768]{1,0:T(8,128)(2,1)} %reduce-scatter.3.cloned.1.call-done) | copy-start | bytes 2359300
  336.8 13.7 %collective-permute-start.18 = (bf16[25,768]{1,0:T(8,128)(2,1)S(1)}, bf16[25,768]{1,0:T(8,128)(2,1)S(1)}, u32[]{:S(2)}, u32[]{:S(2)}) collective-permute-start(bf16[25,768]{1,0:T(8,128)(2,1)S(1)} %get-tuple-element.117), channel_id=1, source_target_pairs={{0,1},{1,2},{2,3},{3,0},{4,5},{5,6},{6,7},{7,4},{8,9},{9,10},{10,1... | collective-permute-start | bytes 115208 | tf_op jit(solution)/shard_map/ppermute | solution.py:336
  338.7 9.2 %collective-permute-start.21 = (bf16[24,768]{1,0:T(8,128)(2,1)S(1)}, bf16[24,768]{1,0:T(8,128)(2,1)S(1)}, u32[]{:S(2)}, u32[]{:S(2)}) collective-permute-start(bf16[24,768]{1,0:T(8,128)(2,1)S(1)} %slice.235), channel_id=1, source_target_pairs={{0,0},{1,8},{2,16},{3,24},{4,1},{5,9},{6,17},{7,25},{8,2},{9,10},{... | collective-permute-start | bytes 110600 | tf_op jit(solution)/shard_map/ppermute | solution.py:504
  342.8 7.9 %collective-permute-start.19 = (bf16[25,768]{1,0:T(8,128)(2,1)S(1)}, bf16[25,768]{1,0:T(8,128)(2,1)S(1)}, u32[]{:S(2)}, u32[]{:S(2)}) collective-permute-start(bf16[25,768]{1,0:T(8,128)(2,1)S(1)} %get-tuple-element.116), channel_id=1, source_target_pairs={{0,2},{1,3},{2,0},{3,1},{4,6},{5,7},{6,4},{7,5},{8,10},{9,11},{10,... | collective-permute-start | bytes 115208 | tf_op jit(solution)/shard_map/ppermute | solution.py:336
  348.0 4.5 %collective-permute-start.20 = (bf16[25,768]{1,0:T(8,128)(2,1)S(1)}, bf16[25,768]{1,0:T(8,128)(2,1)S(1)}, u32[]{:S(2)}, u32[]{:S(2)}) collective-permute-start(bf16[25,768]{1,0:T(8,128)(2,1)S(1)} %get-tuple-element.115), channel_id=1, source_target_pairs={{0,3},{1,0},{2,1},{3,2},{4,7},{5,4},{6,5},{7,6},{8,11},{9,8},{10,9... | collective-permute-start | bytes 115208 | tf_op jit(solution)/shard_map/ppermute | solution.py:336
  350.5 4.4 %copy-start.19 = (f32[512]{0:T(512)S(1)}, f32[512]{0:T(512)}, u32[]{:S(2)}) copy-start(f32[512]{0:T(512)} %copy-done.18) | copy-start | bytes 6148
  350.5 4.4 %copy-start.21 = (f32[512]{0:T(512)S(1)}, f32[512]{0:T(512)}, u32[]{:S(2)}) copy-start(f32[512]{0:T(512)} %add_rsqrt_fusion) | copy-start | bytes 6148
  354.9 2.4 copy-start.3
Sparse Core Ops, SparseCore 0:
  68.2 27.7 all-gather.2
  98.4 33.1 all-gather.4
  183.7 58.4 reduce-scatter.2
  279.0 40.0 reduce-scatter.4
